TPU v7x, 32 devices: a whole 2x2x4 slice. The times are simulated.
32 devices in a mesh: sec: 8 (over y, x, core), img: 4 (over z).
Axes of the slice: x: 2, y: 2, z: 4, core: 2. Of those that a mesh axis runs over, the one named last changes fastest.
Arguments:
- saved_last: bfloat16 [8, 4, 4, 21, 21, 384], P('sec', None, 'img'), may hold values from -6 to 6
- saved_older: bfloat16 [8, 4, 4, 21, 21, 384], P('sec', None, 'img'), may hold values from -6 to 6
- arriving: bfloat16 [8, 2, 4, 21, 21, 384], P('sec', None, 'img'), may hold values from -6 to 6
- head_adjoint: bfloat16 [3, 2, 4, 21, 21, 384], P(None, None, 'img'), may hold values from -6 to 6
- plan: int32 [8, 4], P('sec'), may hold values from 0 to 3, each once within a row
- depth_five: bfloat16 [8, 25, 384], P('sec'), may hold values from -1.25 to 1.25
- depth_three: bfloat16 [8, 9, 384], P('sec'), may hold values from -2 to 2
- point_five: bfloat16 [8, 384, 384], P('sec'), may hold values from -0.3125 to 0.3125
- point_three: bfloat16 [8, 384, 384], P('sec'), may hold values from -0.3125 to 0.3125
Outputs:
- outgoing: bfloat16 [8, 2, 4, 21, 21, 384], P('sec', None, 'img')
- grad_point_five: float32 [8, 384, 384], P('sec', 'img')
- grad_depth_five: float32 [8, 384, 25], P('sec', 'img')
- grad_point_three: float32 [8, 384, 384], P('sec', 'img')
- grad_depth_three: float32 [8, 384, 9], P('sec', 'img')
Inputs may be any that keep to these rules, and one draw needn't show every extreme that they name: `plan`: each row is a permutation of the stash slots.
All inputs are finite; a program needn't handle non-finite values.
Results may differ from a plain program's by a relative error of at most 0.012.
Values may be sent and summed in bfloat16 or wider, within the bound.
A program may use at most 128 MiB of HBM per device.

v0:
```python
import functools

import jax
import jax.numpy as jnp
from jax import lax
from jax.experimental import pallas as pl
from jax.experimental.pallas import tpu as pltpu
from jax.sharding import PartitionSpec as P

F32 = jnp.float32
BF16 = jnp.bfloat16
LANES = 128
WIDE = 256
MESH = pl.DeviceIdType.MESH


def up(value, unit):
    return -(-value // unit) * unit


def turned(block, shift):
    shift = shift % block.shape[0]
    return block if shift == 0 else pltpu.roll(block, shift, 0)


def rows_at(even, odd, pair, offset, lanes):
    if offset % 2 == 0:
        block = even[pair + offset // 2 + 1, :, lanes]
    else:
        block = odd[pair + (offset + 1) // 2, :, lanes]
    return block.reshape(-1, 8, WIDE)


def filtered(even, odd, taps, kernel, pair, lanes, back):
    radius = kernel // 2
    held = [rows_at(even, odd, pair, k - radius, lanes) for k in range(kernel)]
    total = None
    for col_tap in range(kernel):
        part = None
        for row_tap in range(kernel):
            at = kernel - 1 - row_tap if back else row_tap
            term = taps[row_tap * kernel + col_tap, :, lanes][None] * held[at]
            part = term if part is None else part + term
        wide = part.astype(F32).reshape(-1, WIDE)
        moved = turned(wide, col_tap - radius if back else radius - col_tap)
        total = moved if total is None else total + moved
    return total


def tap_sums(even, odd, back, sums, kernel, pair, lanes):
    radius = kernel // 2
    held = [rows_at(even, odd, pair, k - radius, lanes) for k in range(kernel)]
    wide = back[pair + 1, :, lanes].astype(F32)
    for col_tap in range(kernel):
        moved = turned(wide, col_tap - radius).astype(BF16).reshape(-1, 8, WIDE)
        for row_tap in range(kernel):
            term = held[row_tap] * moved
            folded = term[0]
            for part in range(1, term.shape[0]):
                folded = folded + term[part]
            tap = row_tap * kernel + col_tap
            sums[tap, :, lanes] = sums[tap, :, lanes] + folded.astype(F32)


def kernel_body(
    sections,
    group,
    kernels,
    plan,
    last,
    older,
    arriving_last,
    arriving_older,
    head,
    depth_five,
    depth_three,
    point_five,
    point_three,
    outgoing,
    out_five,
    out_three,
    out_taps_five,
    out_taps_three,
    inbox,
    outbox,
    stage,
    even_last,
    odd_last,
    even_older,
    odd_older,
    even_five,
    odd_five,
    even_three,
    odd_three,
    grad_wide,
    grad_flat,
    mixed_five,
    mixed_three,
    taps_five,
    taps_three,
    total_five,
    total_three,
    sums_five,
    sums_three,
    sums_all,
    give_five,
    give_three,
    give_taps,
    take_five,
    take_three,
    take_taps,
    local_sem,
    send_sem,
    recv_sem,
    give_sem,
    take_sem,
):
    five, three = kernels
    turns, height, width, channels = last.shape
    breadth = grad_wide.shape[1]
    rows = channels // group
    factor = 1.0 / (height * width)
    blocks = 2 * channels // WIDE
    columns = channels // LANES
    pairs = grad_wide.shape[0] // 2
    sec = lax.axis_index("sec")
    img = lax.axis_index("img")
    top = sec == sections - 1
    bottom = sec == 0
    not_top = sec < sections - 1
    not_bottom = sec > 0

    def first_copy(which):
        source = (arriving_last, arriving_older)[which]
        target = inbox.at[0, which, pl.ds(0, height)]
        return pltpu.make_async_copy(source, target, local_sem.at[0, which])

    def head_copy(turn, which):
        source = head.at[turn - 1, which]
        target = inbox.at[turn, which, pl.ds(0, height)]
        return pltpu.make_async_copy(source, target, local_sem.at[turn, which])

    for which in range(2):
        first_copy(which).start()

    @pl.when(top)
    def _():
        for turn in range(1, turns):
            for which in range(2):
                head_copy(turn, which).start()

    barrier = pltpu.get_barrier_semaphore()
    for step in range(1, group):
        pl.semaphore_signal(
            barrier,
            inc=1,
            device_id={"sec": sec, "img": lax.rem(img + step, group)},
            device_id_type=MESH,
        )

    @pl.when(not_bottom)
    def _():
        pl.semaphore_signal(
            barrier, inc=1, device_id={"sec": sec - 1, "img": img}, device_id_type=MESH
        )

    @pl.when(not_top)
    def _():
        pl.semaphore_signal(
            barrier, inc=1, device_id={"sec": sec + 1, "img": img}, device_id_type=MESH
        )

    for ref in (sums_five, sums_three, total_five, total_three, sums_all):
        ref[...] = jnp.zeros(ref.shape, ref.dtype)
    edge_even = jnp.zeros(even_five.shape[1:], BF16)
    for ref in (even_last, even_older, even_five, even_three):
        ref[0] = edge_even
        ref[pairs + 1] = edge_even
    for ref in (odd_last, odd_older, odd_five, odd_three):
        ref[pairs] = edge_even
    for row in range(stage.shape[0]):
        stage[row, breadth - 8 : breadth] = jnp.zeros((8, channels), F32)
    for row in range(grad_wide.shape[0]):
        grad_wide[row, breadth - 8 : breadth] = jnp.zeros((8, channels), F32)
    for row in (0, *range(height + 1, stage.shape[0])):
        stage[row] = jnp.zeros((breadth, channels), F32)
    for row in range(height, grad_wide.shape[0]):
        grad_wide[row] = jnp.zeros((breadth, channels), F32)
    for wide, packed in ((depth_five, taps_five), (depth_three, taps_three)):
        for tap in range(packed.shape[0]):
            value = jnp.broadcast_to(wide[tap : tap + 1].astype(F32), (8, channels))
            packed[tap] = jnp.concatenate([value, value], 1).astype(BF16)

    def prepare(turn):
        slot = plan[0, turn]
        for saved, even, odd in ((last, even_last, odd_last), (older, even_older, odd_older)):

            def one(row, carry):
                stage[row + 1, 0:width, :] = jnp.maximum(saved[slot, row].astype(F32), 0.0)
                return carry

            lax.fori_loop(0, height, one, 0, unroll=3)

            def two(pair, carry):
                rows = [stage[2 * pair + k] for k in range(3)]
                odd[pair] = jnp.concatenate(rows[0:2], 1).astype(BF16)
                even[pair + 1] = jnp.concatenate(rows[1:3], 1).astype(BF16)
                return carry

            lax.fori_loop(0, pairs, two, 0)

    def hop(turn, which):
        return pltpu.make_async_remote_copy(
            src_ref=outbox.at[turn, which, pl.ds(0, height)],
            dst_ref=inbox.at[turn + 1, which, pl.ds(0, height)],
            send_sem=send_sem.at[turn, which],
            recv_sem=recv_sem.at[turn, which],
            device_id={"sec": lax.max(sec - 1, 0), "img": img},
            device_id_type=MESH,
        )

    def arrive(turn, which):
        @pl.when(top)
        def _():
            head_copy(turn, which).wait()

        @pl.when(not_top)
        def _():
            hop(turn - 1, which).wait_recv()

    def spread_grad(turn):
        def one(row, carry):
            grad_wide[row, 0:width, :] = inbox[turn, 0, row].astype(F32)
            return carry

        lax.fori_loop(0, height, one, 0, unroll=3)
        grad_flat[...] = grad_wide[0:height].reshape(-1, channels).astype(BF16)

    def pull(weights, even, odd):
        product = lax.dot_general(
            grad_flat[...], weights[...], (((1,), (1,)), ((), ())), preferred_element_type=F32
        )
        zeros = jnp.zeros((breadth, channels), F32)

        def line(row):
            inside = 0 <= row < height
            return product[row * breadth : (row + 1) * breadth] if inside else zeros

        for pair in range(pairs):
            even[pair + 1] = jnp.concatenate([line(2 * pair), line(2 * pair + 1)], 1).astype(BF16)
            odd[pair] = jnp.concatenate([line(2 * pair - 1), line(2 * pair)], 1).astype(BF16)

    def parts(pair, block):
        for part in range(WIDE // LANES):
            at = block * (WIDE // LANES) + part
            lanes = slice((at % columns) * LANES, (at % columns + 1) * LANES)
            yield 2 * pair + at // columns, lanes, slice(part * LANES, (part + 1) * LANES)

    def each_block(work):
        def one(pair, carry):
            for block in range(blocks):
                work(pair, block, slice(block * WIDE, (block + 1) * WIDE))
            return carry

        lax.fori_loop(0, pairs, one, 0)

    def through_five(turn, target):
        def work(pair, block, wide):
            out = filtered(even_five, odd_five, taps_five, five, pair, wide, True)
            kept = jnp.where(even_last[pair + 1, :, wide].astype(F32) > 0, out, 0.0)
            for at, lanes, cut in parts(pair, block):
                extra = inbox[turn, 1, at, :, lanes].astype(F32)
                done = kept[0:width, cut] + grad_wide[at, 0:width, lanes] + extra
                target[at, :, lanes] = done.astype(BF16)

        each_block(work)

    def through_three(target):
        def work(pair, block, wide):
            out = filtered(even_three, odd_three, taps_three, three, pair, wide, True)
            kept = jnp.where(even_older[pair + 1, :, wide].astype(F32) > 0, out, 0.0)
            for at, lanes, cut in parts(pair, block):
                target[at, :, lanes] = kept[0:width, cut].astype(BF16)

        each_block(work)

    def forward():
        def work(pair, block, wide):
            for even, odd, taps, mixed, kernel in (
                (even_last, odd_last, taps_five, mixed_five, five),
                (even_older, odd_older, taps_three, mixed_three, three),
            ):
                out = filtered(even, odd, taps, kernel, pair, wide, False)
                for at, lanes, cut in parts(pair, block):
                    mixed[at, :, lanes] = out[:, cut]

        each_block(work)

    def add_taps():
        def work(pair, block, wide):
            tap_sums(even_last, odd_last, even_five, sums_five, five, pair, wide)
            tap_sums(even_older, odd_older, even_three, sums_three, three, pair, wide)

        each_block(work)

    def add_point(mixed, total):
        flat = mixed[0:height].reshape(-1, channels).astype(BF16)
        total[...] += lax.dot_general(
            flat, grad_flat[...], (((0,), (0,)), ((), ())), preferred_element_type=F32
        )

    def share(part, step):
        source = (give_three, give_five, give_taps)[part]
        target = (take_three, take_five, take_taps)[part]
        peer = lax.rem(img + step, group)
        return pltpu.make_async_remote_copy(
            src_ref=source.at[peer],
            dst_ref=target.at[step],
            send_sem=give_sem.at[part, step],
            recv_sem=take_sem.at[part, step],
            device_id={"sec": sec, "img": peer},
            device_id_type=MESH,
        )

    prepare(0)
    forward()
    callers = group + 1 - bottom.astype(jnp.int32) - top.astype(jnp.int32)
    pl.semaphore_wait(barrier, callers)

    first_copy(0).wait()
    first_copy(1).wait()

    def turn_work(turn, carry):
        spread_grad(turn)
        pull(point_five, even_five, odd_five)

        @pl.when(turn > 0)
        def _():
            arrive(turn, 1)

        through_five(turn, outbox.at[turn, 0])

        @pl.when(not_bottom)
        def _():
            hop(turn, 0).start()

        pull(point_three, even_three, odd_three)
        through_three(outbox.at[turn, 1])

        @pl.when(not_bottom)
        def _():
            hop(turn, 1).start()

        add_point(mixed_five, total_five)
        add_point(mixed_three, total_three)
        add_taps()
        prepare(turn + 1)
        forward()
        arrive(turn + 1, 0)
        return carry

    lax.fori_loop(0, turns - 1, turn_work, 0)

    end = turns - 1
    spread_grad(end)
    for part, mixed, total, give in (
        (0, mixed_three, total_three, give_three),
        (1, mixed_five, total_five, give_five),
    ):
        add_point(mixed, total)
        for peer in range(group):
            give[peer] = (total[peer * rows : (peer + 1) * rows] * factor).astype(BF16)
        for step in range(1, group):
            share(part, step).start()
    pull(point_five, even_five, odd_five)
    pull(point_three, even_three, odd_three)
    add_taps()
    count_five, count_three = five * five, three * three
    for sums, start, count in ((sums_five, 0, count_five), (sums_three, count_five, count_three)):
        folded = jnp.sum(sums[...], axis=1)
        sums_all[start : start + count] = folded[:, 0:channels] + folded[:, channels:]
    flipped = sums_all[...].T * factor
    for peer in range(group):
        give_taps[peer] = flipped[peer * rows : (peer + 1) * rows].astype(BF16)
    for step in range(1, group):
        share(2, step).start()
    arrive(end, 1)
    through_five(end, outgoing.at[0])
    through_three(outgoing.at[1])

    def gathered(part, give, take):
        value = give[img].astype(F32)
        for step in range(1, group):
            share(part, step).wait_recv()
            value = value + take[step].astype(F32)
        return value

    out_three[...] = gathered(0, give_three, take_three)
    out_five[...] = gathered(1, give_five, take_five)
    by_tap = gathered(2, give_taps, take_taps).T
    for tap in range(count_five):
        out_taps_five[tap] = by_tap[tap : tap + 1]
    for tap in range(count_three):
        out_taps_three[tap] = by_tap[count_five + tap : count_five + tap + 1]
    for part in range(3):
        for step in range(1, group):
            share(part, step).wait_send()

    @pl.when(not_bottom)
    def _():
        for turn in range(turns - 1):
            for which in range(2):
                hop(turn, which).wait_send()


def local(
    sections,
    group,
    saved_last,
    saved_older,
    arriving,
    head_adjoint,
    plan,
    depth_five,
    depth_three,
    point_five,
    point_three,
):
    turns, _, height, width, channels = saved_last.shape[1:]
    count_five, count_three = depth_five.shape[1], depth_three.shape[1]
    five, three = round(count_five**0.5), round(count_three**0.5)
    breadth = up(width + five // 2, 8)
    pairs = up(height, 2) // 2
    even = pltpu.VMEM((pairs + 2, breadth, 2 * channels), BF16)
    odd = pltpu.VMEM((pairs + 1, breadth, 2 * channels), BF16)
    rows = channels // group
    vmem = pl.BlockSpec(memory_space=pltpu.VMEM)
    smem = pl.BlockSpec(memory_space=pltpu.SMEM)
    outside = pl.BlockSpec(memory_space=pl.ANY)
    body = functools.partial(kernel_body, sections, group, (five, three))
    outgoing, grad_five, grad_three, taps_five, taps_three = pl.pallas_call(
        body,
        out_shape=(
            jax.ShapeDtypeStruct((2, 2 * pairs, width, channels), BF16),
            jax.ShapeDtypeStruct((rows, channels), F32),
            jax.ShapeDtypeStruct((rows, channels), F32),
            jax.ShapeDtypeStruct((count_five, 1, rows), F32),
            jax.ShapeDtypeStruct((count_three, 1, rows), F32),
        ),
        in_specs=[smem, vmem, vmem, *[outside] * 3, *[vmem] * 4],
        out_specs=(vmem,) * 5,
        scratch_shapes=[
            pltpu.VMEM((turns, 2, 2 * pairs, width, channels), BF16),
            pltpu.VMEM((turns - 1, 2, 2 * pairs, width, channels), BF16),
            pltpu.VMEM((2 * pairs + 2, breadth, channels), F32),
            *([even, odd] * 4),
            pltpu.VMEM((2 * pairs, breadth, channels), F32),
            pltpu.VMEM((height * breadth, channels), BF16),
            pltpu.VMEM((2 * pairs, breadth, channels), F32),
            pltpu.VMEM((2 * pairs, breadth, channels), F32),
            pltpu.VMEM((count_five, 8, 2 * channels), BF16),
            pltpu.VMEM((count_three, 8, 2 * channels), BF16),
            pltpu.VMEM((channels, channels), F32),
            pltpu.VMEM((channels, channels), F32),
            pltpu.VMEM((count_five, 8, 2 * channels), F32),
            pltpu.VMEM((count_three, 8, 2 * channels), F32),
            pltpu.VMEM((LANES, channels), F32),
            pltpu.VMEM((group, rows, channels), BF16),
            pltpu.VMEM((group, rows, channels), BF16),
            pltpu.VMEM((group, rows, LANES), BF16),
            pltpu.VMEM((group, rows, channels), BF16),
            pltpu.VMEM((group, rows, channels), BF16),
            pltpu.VMEM((group, rows, LANES), BF16),
            pltpu.SemaphoreType.DMA((turns, 2)),
            pltpu.SemaphoreType.DMA((turns - 1, 2)),
            pltpu.SemaphoreType.DMA((turns - 1, 2)),
            pltpu.SemaphoreType.DMA((3, group)),
            pltpu.SemaphoreType.DMA((3, group)),
        ],
        compiler_params=pltpu.CompilerParams(collective_id=0, has_side_effects=True),
    )(
        plan,
        saved_last.reshape(turns, height, width, channels),
        saved_older.reshape(turns, height, width, channels),
        arriving[0, 0, 0],
        arriving[0, 1, 0],
        head_adjoint.reshape(turns - 1, 2, height, width, channels),
        depth_five[0],
        depth_three[0],
        point_five[0],
        point_three[0],
    )
    return (
        outgoing[:, :height].reshape(1, 2, 1, height, width, channels),
        grad_five[None],
        taps_five.transpose(1, 2, 0),
        grad_three[None],
        taps_three.transpose(1, 2, 0),
    )


def solution(mesh):
    placed = (
        P("sec", None, "img", None, None, None),
        P("sec", None, "img", None, None, None),
        P("sec", None, "img", None, None, None),
        P(None, None, "img", None, None, None),
        P("sec", None),
        P("sec", None, None),
        P("sec", None, None),
        P("sec", None, None),
        P("sec", None, None),
    )
    return jax.shard_map(
        functools.partial(local, mesh.shape["sec"], mesh.shape["img"]),
        mesh=mesh,
        in_specs=placed,
        out_specs=(
            P("sec", None, "img", None, None, None),
            P("sec", "img", None),
            P("sec", "img", None),
            P("sec", "img", None),
            P("sec", "img", None),
        ),
        check_vma=False,
    )
```

profile of v0, /device:TPU:1, one launch (start us, length us, event | category | flops | bytes accessed | tf_op | source)
XLA Modules:
  0.0 64.6 jit_solution(18223043495930342828)
XLA Ops:
  0.6 2.5 %fusion = (bf16[1,1,1,21,21,384]{5,1,4,3,2,0:T(2,128)(2,1)S(1)}, bf16[1,1,1,21,21,384]{5,1,4,3,2,0:T(2,128)(2,1)S(1)}) fusion(bf16[1,2,1,21,21,384]{5,1,4,3,2,0:T(2,128)(2,1)} %param.11), kind=kLoop, calls=%fused_computation.6 | loop fusion | bytes 1354752 | tf_op jit(solution)/shard_map/slice | solution.py:486
  3.1 0.0 copy-start
  3.1 1.0 %copy_bitcast_fusion.3 = (bf16[21,21,384]{2,1,0:T(8,128)(2,1)}, bf16[21,21,384]{2,1,0:T(8,128)(2,1)}) fusion(bf16[1,1,1,21,21,384]{5,1,4,3,2,0:T(2,128)(2,1)S(1)} %get-tuple-element.20, bf16[1,1,1,21,21,384]{5,1,4,3,2,0:T(2,128)(2,1)S(1)} %get-tuple-element.21), kind=kLoop, calls=%fused_computation.4 | loop fusion | bytes 1354752 | tf_op jit(solution)/shard_map/squeeze | solution.py:486
  4.2 0.8 %copy-done = bf16[3,2,1,21,21,384]{5,1,4,3,2,0:T(2,128)(2,1)S(1)} copy-done((bf16[3,2,1,21,21,384]{5,1,4,3,2,0:T(2,128)(2,1)S(1)}, bf16[3,2,1,21,21,384]{5,1,4,3,2,0:T(2,128)(2,1)}, u32[]{:S(2)}) %copy-start) | copy-done | bytes 2032152
  5.0 0.0 copy-start.1
  5.0 0.0 copy-start.2
  5.0 1.7 %copy.27 = bf16[3,2,1,21,21,384]{5,4,3,1,0,2:T(8,128)(2,1)} copy(bf16[3,2,1,21,21,384]{5,1,4,3,2,0:T(2,128)(2,1)S(1)} %copy-done) | data formatting | bytes 4064256 | tf_op args[3]
  6.7 0.0 copy-done.1
  6.7 0.8 %copy-done.2 = bf16[1,4,1,21,21,384]{5,1,4,3,2,0:T(4,128)(2,1)S(1)} copy-done((bf16[1,4,1,21,21,384]{5,1,4,3,2,0:T(4,128)(2,1)S(1)}, bf16[1,4,1,21,21,384]{5,1,4,3,2,0:T(4,128)(2,1)}, u32[]{:S(2)}) %copy-start.2) | copy-done | bytes 1354776
  7.5 2.1 %copy_bitcast_fusion.1 = (bf16[4,21,21,384]{3,2,1,0:T(8,128)(2,1)}, bf16[4,21,21,384]{3,2,1,0:T(8,128)(2,1)}) fusion(bf16[1,4,1,21,21,384]{5,1,4,3,2,0:T(4,128)(2,1)S(1)} %copy-done.1, bf16[1,4,1,21,21,384]{5,1,4,3,2,0:T(4,128)(2,1)S(1)} %copy-done.2), kind=kLoop, calls=%fused_computation.1 | loop fusion | bytes 5419008 | tf_op jit(solution)/shard_map/reshape | solution.py:484
  9.7 49.7 %shard_map.128 = (bf16[2,22,21,384]{3,2,1,0:T(8,128)(2,1)}, f32[96,384]{1,0:T(8,128)}, f32[96,384]{1,0:T(8,128)}, f32[25,1,96]{2,1,0:T(1,128)}, f32[9,1,96]{2,1,0:T(1,128)}) custom-call(s32[1,4]{1,0:T(1,128)} %plan.1, bf16[4,21,21,384]{3,2,1,0:T(8,128)(2,1)} %get-tuple-element.25.last, bf16[4,21,21,384]{3,2,1,0:T(8,128)(2,1)} %get-tuple-element.24.older, ...), custom_call_target="tpu_custom_call" | custom-call | tf_op jit(solution)/shard_map/pallas_call | solution.py:441
  59.4 0.0 copy-start.4
  59.4 0.0 copy-start.5
  59.4 0.0 copy-start.3
  59.4 0.0 copy-start.6
  59.4 1.3 %slice_bitcast_fusion = bf16[1,2,1,21,21,384]{5,4,3,1,2,0:T(8,128)(2,1)S(1)} fusion(bf16[2,22,21,384]{3,2,1,0:T(8,128)(2,1)} %get-tuple-element.10), kind=kLoop, calls=%fused_computation.3 | loop fusion | bytes 1354752 | tf_op jit(solution)/shard_map/reshape | solution.py:494
  60.7 1.4 %copy.19 = bf16[1,2,1,21,21,384]{5,1,4,3,2,0:T(2,128)(2,1)} copy(bf16[1,2,1,21,21,384]{5,4,3,1,2,0:T(8,128)(2,1)S(1)} %slice_bitcast_fusion) | data formatting | bytes 1354752
  62.1 0.0 copy-done.4
  62.1 0.7 %copy.32 = f32[1,96,384]{2,1,0:T(8,128)} copy(f32[1,96,384]{2,1,0:T(8,128)S(1)} %bitcast.25) | data formatting | bytes 294912
  62.7 0.0 copy-done.5
  62.8 0.6 copy.33
  63.4 0.0 copy-done.3
  63.4 0.7 %copy.34 = f32[1,96,384]{2,1,0:T(8,128)} copy(f32[1,96,384]{2,1,0:T(8,128)S(1)} %bitcast.24) | data formatting | bytes 294912
  64.0 0.0 copy-done.6
  64.0 0.6 copy.35
Async XLA Ops:
  3.1 1.9 %copy-start = (bf16[3,2,1,21,21,384]{5,1,4,3,2,0:T(2,128)(2,1)S(1)}, bf16[3,2,1,21,21,384]{5,1,4,3,2,0:T(2,128)(2,1)}, u32[]{:S(2)}) copy-start(bf16[3,2,1,21,21,384]{5,1,4,3,2,0:T(2,128)(2,1)} %param.12) | copy-start | bytes 6096388
  5.0 1.8 %copy-start.1 = (bf16[1,4,1,21,21,384]{5,1,4,3,2,0:T(4,128)(2,1)S(1)}, bf16[1,4,1,21,21,384]{5,1,4,3,2,0:T(4,128)(2,1)}, u32[]{:S(2)}) copy-start(bf16[1,4,1,21,21,384]{5,1,4,3,2,0:T(4,128)(2,1)} %param.10) | copy-start | bytes 4064260
  5.0 2.6 %copy-start.2 = (bf16[1,4,1,21,21,384]{5,1,4,3,2,0:T(4,128)(2,1)S(1)}, bf16[1,4,1,21,21,384]{5,1,4,3,2,0:T(4,128)(2,1)}, u32[]{:S(2)}) copy-start(bf16[1,4,1,21,21,384]{5,1,4,3,2,0:T(4,128)(2,1)} %param.9) | copy-start | bytes 4064260
  59.4 2.7 %copy-start.4 = (f32[96,384]{1,0:T(8,128)S(1)}, f32[96,384]{1,0:T(8,128)}, u32[]{:S(2)}) copy-start(f32[96,384]{1,0:T(8,128)} %get-tuple-element.11) | copy-start | bytes 442372
  59.4 3.4 %copy-start.5 = (f32[25,1,96]{2,1,0:T(1,128)S(1)}, f32[25,1,96]{2,1,0:T(1,128)}, u32[]{:S(2)}) copy-start(f32[25,1,96]{2,1,0:T(1,128)} %get-tuple-element.12) | copy-start | bytes 28804
  59.4 4.0 %copy-start.3 = (f32[96,384]{1,0:T(8,128)S(1)}, f32[96,384]{1,0:T(8,128)}, u32[]{:S(2)}) copy-start(f32[96,384]{1,0:T(8,128)} %get-tuple-element.13) | copy-start | bytes 442372
  59.4 4.6 %copy-start.6 = (f32[9,1,96]{2,1,0:T(1,128)S(1)}, f32[9,1,96]{2,1,0:T(1,128)}, u32[]{:S(2)}) copy-start(f32[9,1,96]{2,1,0:T(1,128)} %get-tuple-element.14) | copy-start | bytes 10372
where the time goes:
time: 64.9 us; the launch traced here: 64.6 us
  Pallas kernels  49.7 us (77%)
  local copies, waits for them, and re-layouts  14.2 us (22%)
  between operations  0.69 us (1%)
    pallas_call x1, Pallas kernels, local(): pl.pallas_call(body, out_shape=(jax.ShapeDtypeStruct((2, 2 * pairs, width...  49.7 us
    unnamed x20, local copies, waits for them, and re-layouts  7.29 us
    slice x1, local copies, waits for them, and re-layouts, local(): arriving[0, 1, 0]  2.48 us
    reshape x1, local copies, waits for them, and re-layouts, local(): saved_older.reshape(turns, height, width, channels)  2.14 us

commit v1 on v0

v1 whole, which is shorter than its diff:
```python
import functools

import jax
import jax.numpy as jnp
from jax import lax
from jax.experimental import pallas as pl
from jax.experimental.pallas import tpu as pltpu
from jax.sharding import PartitionSpec as P

F32 = jnp.float32
BF16 = jnp.bfloat16
LANES = 128
WIDE = 256
MESH = pl.DeviceIdType.MESH
CHUNKS = 3
GRANT = 36 * 2**20


def up(value, unit):
    return -(-value // unit) * unit


def turned(block, shift):
    shift = shift % block.shape[0]
    return block if shift == 0 else pltpu.roll(block, shift, 0)


def rows_at(even, odd, pair, offset, lanes):
    if offset % 2 == 0:
        block = even[pair + offset // 2 + 1, :, lanes]
    else:
        block = odd[pair + (offset + 1) // 2, :, lanes]
    return block.reshape(-1, 8, WIDE)


def filtered(even, odd, taps, kernel, pair, lanes, back):
    radius = kernel // 2
    held = [rows_at(even, odd, pair, k - radius, lanes) for k in range(kernel)]
    total = None
    for col_tap in range(kernel):
        part = None
        for row_tap in range(kernel):
            at = kernel - 1 - row_tap if back else row_tap
            term = taps[row_tap * kernel + col_tap, :, lanes][None] * held[at]
            part = term if part is None else part + term
        wide = part.astype(F32).reshape(-1, WIDE)
        moved = turned(wide, col_tap - radius if back else radius - col_tap)
        total = moved if total is None else total + moved
    return total


def tap_sums(even, odd, back, sums, kernel, pair, lanes):
    radius = kernel // 2
    held = [rows_at(even, odd, pair, k - radius, lanes) for k in range(kernel)]
    wide = back[pair + 1, :, lanes].astype(F32)
    for col_tap in range(kernel):
        moved = turned(wide, col_tap - radius).astype(BF16).reshape(-1, 8, WIDE)
        for row_tap in range(kernel):
            term = held[row_tap] * moved
            folded = term[0]
            for part in range(1, term.shape[0]):
                folded = folded + term[part]
            tap = row_tap * kernel + col_tap
            sums[tap, :, lanes] = sums[tap, :, lanes] + folded.astype(F32)


def kernel_body(
    sections,
    group,
    kernels,
    spans,
    plan,
    last,
    older,
    arriving,
    head,
    depth_five,
    depth_three,
    point_five,
    point_three,
    outgoing,
    out_five,
    out_three,
    out_taps_five,
    out_taps_three,
    inbox,
    outbox,
    final,
    stage,
    even_last,
    odd_last,
    even_older,
    odd_older,
    even_five,
    odd_five,
    even_three,
    odd_three,
    mixed_five,
    mixed_three,
    taps_five,
    taps_three,
    total_five,
    total_three,
    sums_five,
    sums_three,
    sums_all,
    give_five,
    give_three,
    give_taps,
    take_five,
    take_three,
    take_taps,
    local_sem,
    send_sem,
    recv_sem,
    give_sem,
    take_sem,
    final_sem,
):
    five, three = kernels
    turns, height, width, channels = last.shape
    breadth = stage.shape[1]
    rows = channels // group
    factor = 1.0 / (height * width)
    blocks = 2 * channels // WIDE
    columns = channels // LANES
    pairs = spans[-1][1]
    end = turns - 1
    sec = lax.axis_index("sec")
    img = lax.axis_index("img")
    top = sec == sections - 1
    bottom = sec == 0
    not_top = sec < sections - 1
    not_bottom = sec > 0

    def lines(span):
        return 2 * span[0], min(2 * span[1], height)

    def first_copy(which):
        target = inbox.at[0, which, pl.ds(0, height)]
        return pltpu.make_async_copy(arriving.at[which], target, local_sem.at[0, which])

    def head_copy(turn, which):
        source = head.at[turn - 1, which]
        target = inbox.at[turn, which, pl.ds(0, height)]
        return pltpu.make_async_copy(source, target, local_sem.at[turn, which])

    for which in range(2):
        first_copy(which).start()

    @pl.when(top)
    def _():
        for turn in range(1, turns):
            for which in range(2):
                head_copy(turn, which).start()

    barrier = pltpu.get_barrier_semaphore()
    for step in range(1, group):
        pl.semaphore_signal(
            barrier,
            inc=1,
            device_id={"sec": sec, "img": lax.rem(img + step, group)},
            device_id_type=MESH,
        )

    @pl.when(not_bottom)
    def _():
        pl.semaphore_signal(
            barrier, inc=1, device_id={"sec": sec - 1, "img": img}, device_id_type=MESH
        )

    @pl.when(not_top)
    def _():
        pl.semaphore_signal(
            barrier, inc=1, device_id={"sec": sec + 1, "img": img}, device_id_type=MESH
        )

    edge_even = jnp.zeros(even_five.shape[2:], BF16)

    def clear(turn, carry):
        for ref in (even_last, even_older, even_five, even_three):
            ref[turn, 0] = edge_even
            ref[turn, pairs + 1] = edge_even
        for ref in (odd_last, odd_older, odd_five, odd_three):
            ref[turn, pairs] = edge_even
        return carry

    lax.fori_loop(0, turns, clear, 0)
    for row in range(stage.shape[0]):
        stage[row, breadth - 8 : breadth] = jnp.zeros((8, channels), F32)
    for row in (0, *range(height + 1, stage.shape[0])):
        stage[row] = jnp.zeros((breadth, channels), F32)
    for wide, packed in ((depth_five, taps_five), (depth_three, taps_three)):
        for tap in range(packed.shape[0]):
            value = jnp.broadcast_to(wide[tap : tap + 1].astype(F32), (8, channels))
            packed[tap] = jnp.concatenate([value, value], 1).astype(BF16)

    def prepare(turn):
        slot = plan[0, turn]
        for saved, even, odd in ((last, even_last, odd_last), (older, even_older, odd_older)):

            def one(row, carry):
                stage[row + 1, 0:width, :] = jnp.maximum(saved[slot, row].astype(F32), 0.0)
                return carry

            lax.fori_loop(0, height, one, 0, unroll=3)

            def two(pair, carry):
                rows = [stage[2 * pair + k] for k in range(3)]
                odd[turn, pair] = jnp.concatenate(rows[0:2], 1).astype(BF16)
                even[turn, pair + 1] = jnp.concatenate(rows[1:3], 1).astype(BF16)
                return carry

            lax.fori_loop(0, pairs, two, 0)

    def hop(turn, which, part):
        start, stop = lines(spans[part])
        return pltpu.make_async_remote_copy(
            src_ref=outbox.at[turn, which, pl.ds(start, stop - start)],
            dst_ref=inbox.at[turn + 1, which, pl.ds(start, stop - start)],
            send_sem=send_sem.at[turn, which, part],
            recv_sem=recv_sem.at[turn, which, part],
            device_id={"sec": lax.max(sec - 1, 0), "img": img},
            device_id_type=MESH,
        )

    def arrive(turn, which, part):
        if part == 0:

            @pl.when(jnp.logical_and(turn > 0, top))
            def _():
                head_copy(turn, which).wait()

        @pl.when(jnp.logical_and(turn > 0, not_top))
        def _():
            hop(turn - 1, which, part).wait_recv()

    def pull(turn, part):
        start, stop = lines(spans[part])
        grad = inbox[turn, 0, start:stop].reshape(-1, channels)
        for weights, even, odd in (
            (point_five, even_five, odd_five),
            (point_three, even_three, odd_three),
        ):
            product = lax.dot_general(
                grad, weights[...], (((1,), (1,)), ((), ())), preferred_element_type=F32
            )

            def line(row):
                if start <= row < stop:
                    at = (row - start) * breadth
                    return product[at : at + breadth].astype(BF16)
                if 0 < row < start:
                    return even[turn, row // 2 + 1, :, (row % 2) * channels : (row % 2 + 1) * channels]
                return jnp.zeros((breadth, channels), BF16)

            for pair in range(*spans[part]):
                for side in range(2):
                    lanes = slice(side * channels, (side + 1) * channels)
                    even[turn, pair + 1, :, lanes] = line(2 * pair + side)
                    odd[turn, pair, :, lanes] = line(2 * pair - 1 + side)

    def parts(pair, block):
        for part in range(WIDE // LANES):
            at = block * (WIDE // LANES) + part
            lanes = slice((at % columns) * LANES, (at % columns + 1) * LANES)
            yield 2 * pair + at // columns, lanes, slice(part * LANES, (part + 1) * LANES)

    def each_block(work, span):
        def one(pair, carry):
            for block in range(blocks):
                work(pair, block, slice(block * WIDE, (block + 1) * WIDE))
            return carry

        lax.fori_loop(span[0], span[1], one, 0)

    def through_five(turn, target, span):
        wide_to = target.shape[1]

        def work(pair, block, wide):
            out = filtered(
                even_five.at[turn], odd_five.at[turn], taps_five, five, pair, wide, True
            )
            kept = jnp.where(even_last[turn, pair + 1, :, wide].astype(F32) > 0, out, 0.0)
            for at, lanes, cut in parts(pair, block):
                own = inbox[turn, 0, at, :, lanes].astype(F32)
                extra = inbox[turn, 1, at, :, lanes].astype(F32)
                done = kept[:, cut] + own + extra
                target[at, :, lanes] = done[0:wide_to].astype(BF16)

        each_block(work, span)

    def through_three(turn, target, span):
        wide_to = target.shape[1]

        def work(pair, block, wide):
            out = filtered(
                even_three.at[turn], odd_three.at[turn], taps_three, three, pair, wide, True
            )
            kept = jnp.where(even_older[turn, pair + 1, :, wide].astype(F32) > 0, out, 0.0)
            for at, lanes, cut in parts(pair, block):
                target[at, :, lanes] = kept[0:wide_to, cut].astype(BF16)

        each_block(work, span)

    def forward(turn, span):
        def work(pair, block, wide):
            for even, odd, taps, mixed, kernel in (
                (even_last, odd_last, taps_five, mixed_five, five),
                (even_older, odd_older, taps_three, mixed_three, three),
            ):
                out = filtered(even.at[turn], odd.at[turn], taps, kernel, pair, wide, False)
                for at, lanes, cut in parts(pair, block):
                    mixed[at, :, lanes] = out[:, cut].astype(BF16)

        each_block(work, span)

    def add_taps(turn):
        def work(pair, block, wide):
            tap_sums(
                even_last.at[turn], odd_last.at[turn], even_five.at[turn], sums_five, five, pair, wide
            )
            tap_sums(
                even_older.at[turn], odd_older.at[turn], even_three.at[turn], sums_three, three, pair, wide
            )

        each_block(work, (0, pairs))

    def add_point(turn, mixed, total):
        flat = mixed[0:height].reshape(-1, channels)
        grad = inbox[turn, 0, 0:height].reshape(-1, channels)
        total[...] += lax.dot_general(
            flat, grad, (((0,), (0,)), ((), ())), preferred_element_type=F32
        )

    def share(part, step):
        source = (give_three, give_five, give_taps)[part]
        target = (take_three, take_five, take_taps)[part]
        peer = lax.rem(img + step, group)
        return pltpu.make_async_remote_copy(
            src_ref=source.at[peer],
            dst_ref=target.at[step],
            send_sem=give_sem.at[part, step],
            recv_sem=take_sem.at[part, step],
            device_id={"sec": sec, "img": peer},
            device_id_type=MESH,
        )

    prepare(0)
    callers = group + 1 - bottom.astype(jnp.int32) - top.astype(jnp.int32)
    pl.semaphore_wait(barrier, callers)
    for ref in (sums_five, sums_three, total_five, total_three, sums_all):
        ref[...] = jnp.zeros(ref.shape, ref.dtype)
    first_copy(0).wait()
    first_copy(1).wait()

    def turn_work(turn, carry):
        def ready(part):
            arrive(turn, 1, part)
            for which, through in ((0, through_five), (1, through_three)):
                through(turn, outbox.at[turn, which], spans[part])

                @pl.when(not_bottom)
                def _():
                    hop(turn, which, part).start()

        for part in range(len(spans)):
            arrive(turn, 0, part)
            pull(turn, part)
            if part > 0:
                ready(part - 1)
            if part + 1 < len(spans):
                forward(turn, spans[part])
        ready(len(spans) - 1)
        forward(turn, spans[-1])
        add_point(turn, mixed_five, total_five)
        add_point(turn, mixed_three, total_three)
        prepare(turn + 1)
        return carry

    lax.fori_loop(0, end, turn_work, 0)

    forward(end, (0, pairs))
    for part in range(len(spans)):
        arrive(end, 0, part)
    for part, mixed, total, give in (
        (0, mixed_three, total_three, give_three),
        (1, mixed_five, total_five, give_five),
    ):
        add_point(end, mixed, total)
        for peer in range(group):
            give[peer] = (total[peer * rows : (peer + 1) * rows] * factor).astype(BF16)
        for step in range(1, group):
            share(part, step).start()
    for part in range(len(spans)):
        pull(end, part)

    def all_taps(turn, carry):
        add_taps(turn)
        return carry

    lax.fori_loop(0, turns, all_taps, 0)
    count_five, count_three = five * five, three * three
    for sums, start, count in ((sums_five, 0, count_five), (sums_three, count_five, count_three)):
        folded = jnp.sum(sums[...], axis=1)
        sums_all[start : start + count] = folded[:, 0:channels] + folded[:, channels:]
    flipped = sums_all[...].T * factor
    for peer in range(group):
        give_taps[peer] = flipped[peer * rows : (peer + 1) * rows].astype(BF16)
    for step in range(1, group):
        share(2, step).start()
    for part in range(len(spans)):
        arrive(end, 1, part)
    through_five(end, final.at[0], (0, pairs))
    through_three(end, final.at[1], (0, pairs))
    finals = [
        pltpu.make_async_copy(
            final.at[which, pl.ds(0, height)], outgoing.at[which], final_sem.at[which]
        )
        for which in range(2)
    ]
    for copy in finals:
        copy.start()

    def gathered(part, give, take):
        value = give[img].astype(F32)
        for step in range(1, group):
            share(part, step).wait_recv()
            value = value + take[step].astype(F32)
        return value

    out_three[...] = gathered(0, give_three, take_three)
    out_five[...] = gathered(1, give_five, take_five)
    by_tap = gathered(2, give_taps, take_taps).T
    for tap in range(count_five):
        out_taps_five[tap] = by_tap[tap : tap + 1]
    for tap in range(count_three):
        out_taps_three[tap] = by_tap[count_five + tap : count_five + tap + 1]
    for part in range(3):
        for step in range(1, group):
            share(part, step).wait_send()
    for copy in finals:
        copy.wait()

    @pl.when(not_bottom)
    def _():
        for turn in range(end):
            for which in range(2):
                for part in range(len(spans)):
                    hop(turn, which, part).wait_send()


def local(
    sections,
    group,
    saved_last,
    saved_older,
    arriving,
    head_adjoint,
    plan,
    depth_five,
    depth_three,
    point_five,
    point_three,
):
    turns, _, height, width, channels = saved_last.shape[1:]
    count_five, count_three = depth_five.shape[1], depth_three.shape[1]
    five, three = round(count_five**0.5), round(count_three**0.5)
    breadth = up(width + five // 2, 8)
    pairs = up(height, 2) // 2
    even = pltpu.VMEM((turns, pairs + 2, breadth, 2 * channels), BF16)
    odd = pltpu.VMEM((turns, pairs + 1, breadth, 2 * channels), BF16)
    rows = channels // group
    chunk = -(-pairs // CHUNKS)
    spans = tuple((at, min(at + chunk, pairs)) for at in range(0, pairs, chunk))
    vmem = pl.BlockSpec(memory_space=pltpu.VMEM)
    smem = pl.BlockSpec(memory_space=pltpu.SMEM)
    outside = pl.BlockSpec(memory_space=pl.ANY)
    body = functools.partial(kernel_body, sections, group, (five, three), spans)
    grow = (0, breadth - width)
    outgoing, grad_five, grad_three, taps_five, taps_three = pl.pallas_call(
        body,
        out_shape=(
            jax.ShapeDtypeStruct((2, height, width, channels), BF16),
            jax.ShapeDtypeStruct((rows, channels), F32),
            jax.ShapeDtypeStruct((rows, channels), F32),
            jax.ShapeDtypeStruct((count_five, 1, rows), F32),
            jax.ShapeDtypeStruct((count_three, 1, rows), F32),
        ),
        in_specs=[smem, vmem, vmem, *[outside] * 2, *[vmem] * 4],
        out_specs=(outside, *[vmem] * 4),
        scratch_shapes=[
            pltpu.VMEM((turns, 2, 2 * pairs, breadth, channels), BF16),
            pltpu.VMEM((turns - 1, 2, 2 * pairs, breadth, channels), BF16),
            pltpu.VMEM((2, 2 * pairs, width, channels), BF16),
            pltpu.VMEM((2 * pairs + 2, breadth, channels), F32),
            *([even, odd] * 4),
            pltpu.VMEM((2 * pairs, breadth, channels), BF16),
            pltpu.VMEM((2 * pairs, breadth, channels), BF16),
            pltpu.VMEM((count_five, 8, 2 * channels), BF16),
            pltpu.VMEM((count_three, 8, 2 * channels), BF16),
            pltpu.VMEM((channels, channels), F32),
            pltpu.VMEM((channels, channels), F32),
            pltpu.VMEM((count_five, 8, 2 * channels), F32),
            pltpu.VMEM((count_three, 8, 2 * channels), F32),
            pltpu.VMEM((LANES, channels), F32),
            pltpu.VMEM((group, rows, channels), BF16),
            pltpu.VMEM((group, rows, channels), BF16),
            pltpu.VMEM((group, rows, LANES), BF16),
            pltpu.VMEM((group, rows, channels), BF16),
            pltpu.VMEM((group, rows, channels), BF16),
            pltpu.VMEM((group, rows, LANES), BF16),
            pltpu.SemaphoreType.DMA((turns, 2)),
            pltpu.SemaphoreType.DMA((turns - 1, 2, len(spans))),
            pltpu.SemaphoreType.DMA((turns - 1, 2, len(spans))),
            pltpu.SemaphoreType.DMA((3, group)),
            pltpu.SemaphoreType.DMA((3, group)),
            pltpu.SemaphoreType.DMA((2,)),
        ],
        compiler_params=pltpu.CompilerParams(
            collective_id=0, has_side_effects=True, vmem_limit_bytes=GRANT
        ),
    )(
        plan,
        saved_last.reshape(turns, height, width, channels),
        saved_older.reshape(turns, height, width, channels),
        jnp.pad(arriving[0, :, 0], ((0, 0), (0, 0), grow, (0, 0))),
        jnp.pad(head_adjoint[:, :, 0], ((0, 0), (0, 0), (0, 0), grow, (0, 0))),
        depth_five[0],
        depth_three[0],
        point_five[0],
        point_three[0],
    )
    return (
        outgoing.reshape(1, 2, 1, height, width, channels),
        grad_five[None],
        taps_five.transpose(1, 2, 0),
        grad_three[None],
        taps_three.transpose(1, 2, 0),
    )


def solution(mesh):
    placed = (
        P("sec", None, "img", None, None, None),
        P("sec", None, "img", None, None, None),
        P("sec", None, "img", None, None, None),
        P(None, None, "img", None, None, None),
        P("sec", None),
        P("sec", None, None),
        P("sec", None, None),
        P("sec", None, None),
        P("sec", None, None),
    )
    return jax.shard_map(
        functools.partial(local, mesh.shape["sec"], mesh.shape["img"]),
        mesh=mesh,
        in_specs=placed,
        out_specs=(
            P("sec", None, "img", None, None, None),
            P("sec", "img", None),
            P("sec", "img", None),
            P("sec", "img", None),
            P("sec", "img", None),
        ),
        check_vma=False,
    )
```

time: 64.9 us -> 57.1 us (0.88)
  local copies, waits for them, and re-layouts: 14.2 us -> 8.73 us
  Pallas kernels: 49.7 us -> 47.5 us
    slice x1 -> x0, local copies, waits for them, and re-layouts: 2.48 us -> none  [local(): arriving[0, 1, 0]]
    pallas_call x1, Pallas kernels: 49.7 us -> 47.5 us  [local(): pl.pallas_call(body, out_shape=(jax.ShapeDtypeStruct((2, height, width, c...]
    reshape x1, local copies, waits for them, and re-layouts: 2.14 us -> 0.45 us  [local(): saved_older.reshape(turns, height, width, channels)]
    reshape x1 -> x0, local copies, waits for them, and re-layouts: 1.28 us -> none  [local(): outgoing[:, :height].reshape(1, 2, 1, height, width, channels)]
    squeeze x1 -> x0, local copies, waits for them, and re-layouts: 1.03 us -> none  [local(): arriving[0, 1, 0]]
    unnamed x20 -> x23, local copies, waits for them, and re-layouts: 7.29 us -> 7.93 us
where the time goes in v1:
time: 57.1 us; the launch traced here: 56.9 us
  Pallas kernels  47.5 us (83%)
  local copies, waits for them, and re-layouts  8.73 us (15%)
  between operations  0.71 us (1%)
    pallas_call x1, Pallas kernels, local(): pl.pallas_call(body, out_shape=(jax.ShapeDtypeStruct((2, height, width, c...  47.5 us
    unnamed x23, local copies, waits for them, and re-layouts  7.93 us

profile of v1, /device:TPU:1, one launch (start us, length us, event | category | flops | bytes accessed | tf_op | source)
XLA Modules:
  0.0 56.9 jit_solution(510425861837936365)
XLA Ops:
  0.6 0.0 copy-start.5
  0.6 1.3 %copy.24 = bf16[1,2,1,21,21,384]{5,4,3,1,2,0:T(8,128)(2,1)S(1)} copy(bf16[1,2,1,21,21,384]{5,1,4,3,2,0:T(2,128)(2,1)} %param.11) | data formatting | bytes 1354752 | tf_op args[2]
  2.0 0.1 pad.8.arriving
  2.1 0.3 copy-done.5
  2.4 0.3 copy.23
  2.7 0.0 copy-start.6
  2.7 0.0 copy-start.7
  2.8 0.3 pad.9.head
  3.0 1.0 %copy-done.6 = bf16[1,4,1,21,21,384]{5,1,4,3,2,0:T(4,128)(2,1)S(1)} copy-done((bf16[1,4,1,21,21,384]{5,1,4,3,2,0:T(4,128)(2,1)S(1)}, bf16[1,4,1,21,21,384]{5,1,4,3,2,0:T(4,128)(2,1)}, u32[]{:S(2)}) %copy-start.6) | copy-done | bytes 1354776
  4.1 0.4 copy-done.7
  4.5 0.0 copy-start
  4.5 0.0 copy-start.1
  4.5 0.0 copy-start.2
  4.5 0.0 copy-start.3
  4.5 0.0 copy-start.4
  4.5 0.4 copy_bitcast_fusion.1
  5.0 0.5 copy-done
  5.4 0.1 copy-done.1
  5.5 0.0 copy-done.2
  5.5 0.0 copy-done.3
  5.5 0.0 copy-done.4
  5.5 47.5 %shard_map.128 = (bf16[2,21,21,384]{3,2,1,0:T(8,128)(2,1)S(1)}, f32[96,384]{1,0:T(8,128)S(1)}, f32[96,384]{1,0:T(8,128)S(1)}, f32[25,1,96]{2,1,0:T(1,128)S(1)}, f32[9,1,96]{2,1,0:T(1,128)S(1)}) custom-call(s32[1,4]{1,0:T(1,128)S(1)} %copy-done.4, bf16[4,21,21,384]{3,2,1,0:T(8,128)(2,1)S(1)} %get-tuple-element.21.last, ...), custom_call_target="tpu_custom_call" | custom-call | tf_op jit(solution)/shard_map/pallas_call | solution.py:481
  53.0 1.4 %copy.18 = bf16[1,2,1,21,21,384]{5,1,4,3,2,0:T(2,128)(2,1)} copy(bf16[1,2,1,21,21,384]{5,4,3,1,2,0:T(8,128)(2,1)S(1)} %bitcast.19) | data formatting | bytes 1354752
  54.4 0.7 %copy.29 = f32[1,96,384]{2,1,0:T(8,128)} copy(f32[1,96,384]{2,1,0:T(8,128)S(1)} %bitcast.23) | data formatting | bytes 294912
  55.1 0.6 %copy.30 = f32[1,96,25]{1,0,2:T(1,128)} copy(f32[1,96,25]{1,0,2:T(1,128)S(1)} %bitcast.25) | data formatting | bytes 19200
  55.7 0.7 %copy.31 = f32[1,96,384]{2,1,0:T(8,128)} copy(f32[1,96,384]{2,1,0:T(8,128)S(1)} %bitcast.22) | data formatting | bytes 294912
  56.3 0.6 %copy.32 = f32[1,96,9]{1,0,2:T(1,128)} copy(f32[1,96,9]{1,0,2:T(1,128)S(1)} %bitcast.27) | data formatting | bytes 6912
Async XLA Ops:
  0.6 1.8 %copy-start.5 = (bf16[3,2,1,21,21,384]{5,1,4,3,2,0:T(2,128)(2,1)S(1)}, bf16[3,2,1,21,21,384]{5,1,4,3,2,0:T(2,128)(2,1)}, u32[]{:S(2)}) copy-start(bf16[3,2,1,21,21,384]{5,1,4,3,2,0:T(2,128)(2,1)} %param.12) | copy-start | bytes 6096388
  2.7 1.3 %copy-start.6 = (bf16[1,4,1,21,21,384]{5,1,4,3,2,0:T(4,128)(2,1)S(1)}, bf16[1,4,1,21,21,384]{5,1,4,3,2,0:T(4,128)(2,1)}, u32[]{:S(2)}) copy-start(bf16[1,4,1,21,21,384]{5,1,4,3,2,0:T(4,128)(2,1)} %param.10) | copy-start | bytes 4064260
  2.7 1.7 %copy-start.7 = (bf16[1,4,1,21,21,384]{5,1,4,3,2,0:T(4,128)(2,1)S(1)}, bf16[1,4,1,21,21,384]{5,1,4,3,2,0:T(4,128)(2,1)}, u32[]{:S(2)}) copy-start(bf16[1,4,1,21,21,384]{5,1,4,3,2,0:T(4,128)(2,1)} %param.9) | copy-start | bytes 4064260
  4.5 1.0 %copy-start = (bf16[1,384,384]{2,1,0:T(8,128)(2,1)S(1)}, bf16[1,384,384]{2,1,0:T(8,128)(2,1)}, u32[]{:S(2)}) copy-start(bf16[1,384,384]{2,1,0:T(8,128)(2,1)} %param.16) | copy-start | bytes 884740
  4.5 1.0 %copy-start.1 = (bf16[1,384,384]{2,1,0:T(8,128)(2,1)S(1)}, bf16[1,384,384]{2,1,0:T(8,128)(2,1)}, u32[]{:S(2)}) copy-start(bf16[1,384,384]{2,1,0:T(8,128)(2,1)} %param.17) | copy-start | bytes 884740
  4.5 1.0 %copy-start.2 = (bf16[1,25,384]{2,1,0:T(8,128)(2,1)S(1)}, bf16[1,25,384]{2,1,0:T(8,128)(2,1)}, u32[]{:S(2)}) copy-start(bf16[1,25,384]{2,1,0:T(8,128)(2,1)} %param.14) | copy-start | bytes 57604
  4.5 1.0 %copy-start.3 = (bf16[1,9,384]{2,1,0:T(8,128)(2,1)S(1)}, bf16[1,9,384]{2,1,0:T(8,128)(2,1)}, u32[]{:S(2)}) copy-start(bf16[1,9,384]{2,1,0:T(8,128)(2,1)} %param.15) | copy-start | bytes 20740
  4.5 1.0 %copy-start.4 = (s32[1,4]{1,0:T(1,128)S(1)}, s32[1,4]{1,0:T(1,128)}, u32[]{:S(2)}) copy-start(s32[1,4]{1,0:T(1,128)} %plan.1) | copy-start | bytes 52

commit v2 on v1

--- a/solution.py
+++ b/solution.py
@@ -2,6 +2,7 @@
 
 import jax
 import jax.numpy as jnp
+import numpy as np
 from jax import lax
 from jax.experimental import pallas as pl
 from jax.experimental.pallas import tpu as pltpu
@@ -12,6 +13,7 @@
 LANES = 128
 WIDE = 256
 MESH = pl.DeviceIdType.MESH
+TWO = 2
 CHUNKS = 3
 GRANT = 36 * 2**20
 
@@ -33,7 +35,7 @@
     return block.reshape(-1, 8, WIDE)
 
 
-def filtered(even, odd, taps, kernel, pair, lanes, back):
+def rolled(even, odd, taps, kernel, pair, lanes, back):
     radius = kernel // 2
     held = [rows_at(even, odd, pair, k - radius, lanes) for k in range(kernel)]
     total = None
@@ -47,6 +49,75 @@
         moved = turned(wide, col_tap - radius if back else radius - col_tap)
         total = moved if total is None else total + moved
     return total
+
+
+def filtered(even, odd, taps, kernel, group, select, parts, back):
+    radius = kernel // 2
+    breadth, wides = even.shape[1:]
+    for slot, pair in enumerate(group):
+        for first in range(0, wides, WIDE):
+            lanes = slice(first, first + WIDE)
+            held = [rows_at(even, odd, pair, k - radius, lanes) for k in range(kernel)]
+            for col_tap in range(kernel):
+                part = None
+                for row_tap in range(kernel):
+                    at = kernel - 1 - row_tap if back else row_tap
+                    term = taps[row_tap * kernel + col_tap, :, lanes][None] * held[at]
+                    part = term if part is None else part + term
+                at = slot * LANES + col_tap * breadth
+                parts[at : at + breadth, lanes] = part.reshape(breadth, WIDE)
+    return lax.dot_general(
+        select[...], parts[...], (((1,), (0,)), ((), ())), preferred_element_type=F32
+    )
+
+
+def selection(breadth, width, kernel, back):
+    table = np.zeros((TWO * breadth, TWO * LANES), np.float32)
+    for slot in range(TWO):
+        for col_tap in range(kernel):
+            shift = kernel // 2 - col_tap if back else col_tap - kernel // 2
+            for col in range(width):
+                if 0 <= col + shift < width:
+                    at = slot * LANES + col_tap * breadth + col + shift
+                    table[slot * breadth + col, at] = 1.0
+    return jnp.asarray(table, BF16)
+
+
+def tap_folds(even, odd, back, folds, kernel, pair):
+    radius = kernel // 2
+    breadth, wides = even.shape[1:]
+    for first in range(0, wides, WIDE):
+        lanes = slice(first, first + WIDE)
+        held = [rows_at(even, odd, pair, k - radius, lanes) for k in range(kernel)]
+        wide = back[pair + 1, :, lanes].astype(F32)
+        for col_tap in range(kernel):
+            other = turned(wide, col_tap - radius).astype(BF16).reshape(-1, 8, WIDE)
+            for row_tap in range(kernel):
+                term = held[row_tap] * other
+                folded = term[0]
+                for part in range(1, term.shape[0]):
+                    folded = folded + term[part]
+                tap = row_tap * kernel + col_tap
+                folds[tap * 8 : tap * 8 + 8, lanes] = folded
+
+
+def gathering(count):
+    table = np.zeros((up(count, 8), up(count * 8, LANES)), np.float32)
+    for tap in range(count):
+        table[tap, tap * 8 : tap * 8 + 8] = 1.0
+    return jnp.asarray(table, BF16)
+
+
+def selection(breadth, width, kernel, back):
+    table = np.zeros((TWO * breadth, TWO * LANES), np.float32)
+    for slot in range(TWO):
+        for col_tap in range(kernel):
+            shift = kernel // 2 - col_tap if back else col_tap - kernel // 2
+            for col in range(width):
+                if 0 <= col + shift < width:
+                    at = slot * LANES + col_tap * breadth + col + shift
+                    table[slot * breadth + col, at] = 1.0
+    return jnp.asarray(table, BF16)
 
 
 def tap_sums(even, odd, back, sums, kernel, pair, lanes):
@@ -78,6 +149,12 @@
     depth_three,
     point_five,
     point_three,
+    select_five,
+    select_three,
+    select_five_back,
+    select_three_back,
+    gather_five,
+    gather_three,
     outgoing,
     out_five,
     out_three,
@@ -86,7 +163,6 @@
     inbox,
     outbox,
     final,
-    stage,
     even_last,
     odd_last,
     even_older,
@@ -97,6 +173,11 @@
     odd_three,
     mixed_five,
     mixed_three,
+    parts_five,
+    parts_three,
+    point_both,
+    folds_five,
+    folds_three,
     taps_five,
     taps_three,
     total_five,
@@ -110,6 +191,8 @@
     take_five,
     take_three,
     take_taps,
+    relay_three,
+    relay_five,
     local_sem,
     send_sem,
     recv_sem,
@@ -119,13 +202,14 @@
 ):
     five, three = kernels
     turns, height, width, channels = last.shape
-    breadth = stage.shape[1]
+    breadth = inbox.shape[3]
     rows = channels // group
     factor = 1.0 / (height * width)
+    pairs = spans[-1][1]
     blocks = 2 * channels // WIDE
     columns = channels // LANES
-    pairs = spans[-1][1]
     end = turns - 1
+    folded = group == 4
     sec = lax.axis_index("sec")
     img = lax.axis_index("img")
     top = sec == sections - 1
@@ -186,10 +270,6 @@
         return carry
 
     lax.fori_loop(0, turns, clear, 0)
-    for row in range(stage.shape[0]):
-        stage[row, breadth - 8 : breadth] = jnp.zeros((8, channels), F32)
-    for row in (0, *range(height + 1, stage.shape[0])):
-        stage[row] = jnp.zeros((breadth, channels), F32)
     for wide, packed in ((depth_five, taps_five), (depth_three, taps_three)):
         for tap in range(packed.shape[0]):
             value = jnp.broadcast_to(wide[tap : tap + 1].astype(F32), (8, channels))
@@ -197,21 +277,21 @@
 
     def prepare(turn):
         slot = plan[0, turn]
+        zeros = jnp.zeros((breadth, channels), BF16)
+        edge = jnp.zeros((breadth - width, channels), F32)
         for saved, even, odd in ((last, even_last, odd_last), (older, even_older, odd_older)):
-
-            def one(row, carry):
-                stage[row + 1, 0:width, :] = jnp.maximum(saved[slot, row].astype(F32), 0.0)
-                return carry
-
-            lax.fori_loop(0, height, one, 0, unroll=3)
-
-            def two(pair, carry):
-                rows = [stage[2 * pair + k] for k in range(3)]
-                odd[turn, pair] = jnp.concatenate(rows[0:2], 1).astype(BF16)
-                even[turn, pair + 1] = jnp.concatenate(rows[1:3], 1).astype(BF16)
-                return carry
-
-            lax.fori_loop(0, pairs, two, 0)
+            for row in range(-1, 2 * pairs):
+                inside = 0 <= row < height
+                active = zeros
+                if inside:
+                    raised = jnp.maximum(saved[slot, row], 0).astype(F32)
+                    active = jnp.concatenate([raised, edge], 0).astype(BF16)
+                lanes = slice((row % 2) * channels, (row % 2 + 1) * channels)
+                if row >= 0:
+                    even[turn, row // 2 + 1, :, lanes] = active
+                if row < 2 * pairs - 1:
+                    lanes = slice((1 - row % 2) * channels, (2 - row % 2) * channels)
+                    odd[turn, (row + 1) // 2, :, lanes] = active
 
     def hop(turn, which, part):
         start, stop = lines(spans[part])
@@ -235,26 +315,23 @@
         def _():
             hop(turn - 1, which, part).wait_recv()
 
-    def pull(turn, part):
-        start, stop = lines(spans[part])
-        grad = inbox[turn, 0, start:stop].reshape(-1, channels)
-        for weights, even, odd in (
-            (point_five, even_five, odd_five),
-            (point_three, even_three, odd_three),
+    def pull(turn):
+        grad = inbox[turn, 0, 0:height].reshape(-1, channels)
+        product = lax.dot_general(
+            grad, point_both[...], (((1,), (1,)), ((), ())), preferred_element_type=F32
+        )
+        for even, odd, first in (
+            (even_five, odd_five, 0),
+            (even_three, odd_three, channels),
         ):
-            product = lax.dot_general(
-                grad, weights[...], (((1,), (1,)), ((), ())), preferred_element_type=F32
-            )
 
             def line(row):
-                if start <= row < stop:
-                    at = (row - start) * breadth
-                    return product[at : at + breadth].astype(BF16)
-                if 0 < row < start:
-                    return even[turn, row // 2 + 1, :, (row % 2) * channels : (row % 2 + 1) * channels]
+                if 0 <= row < height:
+                    at = row * breadth
+                    return product[at : at + breadth, first : first + channels].astype(BF16)
                 return jnp.zeros((breadth, channels), BF16)
 
-            for pair in range(*spans[part]):
+            for pair in range(pairs):
                 for side in range(2):
                     lanes = slice(side * channels, (side + 1) * channels)
                     even[turn, pair + 1, :, lanes] = line(2 * pair + side)
@@ -274,11 +351,11 @@
 
         lax.fori_loop(span[0], span[1], one, 0)
 
-    def through_five(turn, target, span):
+    def compact_five(turn, target, span):
         wide_to = target.shape[1]
 
         def work(pair, block, wide):
-            out = filtered(
+            out = rolled(
                 even_five.at[turn], odd_five.at[turn], taps_five, five, pair, wide, True
             )
             kept = jnp.where(even_last[turn, pair + 1, :, wide].astype(F32) > 0, out, 0.0)
@@ -290,11 +367,11 @@
 
         each_block(work, span)
 
-    def through_three(turn, target, span):
+    def compact_three(turn, target, span):
         wide_to = target.shape[1]
 
         def work(pair, block, wide):
-            out = filtered(
+            out = rolled(
                 even_three.at[turn], odd_three.at[turn], taps_three, three, pair, wide, True
             )
             kept = jnp.where(even_older[turn, pair + 1, :, wide].astype(F32) > 0, out, 0.0)
@@ -303,28 +380,74 @@
 
         each_block(work, span)
 
+    def groups(span):
+        for count, first in enumerate(range(span[0], span[1], TWO)):
+            yield count % 2, range(first, min(first + TWO, span[1]))
+
+    def sides(group, out):
+        for slot, pair in enumerate(group):
+            for side in range(2):
+                lanes = slice(side * channels, (side + 1) * channels)
+                at = slot * breadth
+                yield pair, 2 * pair + side, lanes, out[at : at + breadth, lanes]
+
+    def through_five(turn, target, span):
+        wide_to = target.shape[1]
+        for odds, group in groups(span):
+            out = filtered(
+                even_five.at[turn],
+                odd_five.at[turn],
+                taps_five,
+                five,
+                group,
+                select_five_back,
+                parts_five.at[odds],
+                True,
+            )
+            for pair, row, lanes, value in sides(group, out):
+                kept = jnp.where(even_last[turn, pair + 1, :, lanes].astype(F32) > 0, value, 0.0)
+                own = inbox[turn, 0, row].astype(F32)
+                extra = inbox[turn, 1, row].astype(F32)
+                target[row] = (kept + own + extra)[0:wide_to].astype(BF16)
+
+    def through_three(turn, target, span):
+        wide_to = target.shape[1]
+        for odds, group in groups(span):
+            out = filtered(
+                even_three.at[turn],
+                odd_three.at[turn],
+                taps_three,
+                three,
+                group,
+                select_three_back,
+                parts_three.at[odds],
+                True,
+            )
+            for pair, row, lanes, value in sides(group, out):
+                kept = jnp.where(even_older[turn, pair + 1, :, lanes].astype(F32) > 0, value, 0.0)
+                target[row] = kept[0:wide_to].astype(BF16)
+
     def forward(turn, span):
-        def work(pair, block, wide):
-            for even, odd, taps, mixed, kernel in (
-                (even_last, odd_last, taps_five, mixed_five, five),
-                (even_older, odd_older, taps_three, mixed_three, three),
+        for odds, group in groups(span):
+            for even, odd, taps, mixed, kernel, select, held in (
+                (even_last, odd_last, taps_five, mixed_five, five, select_five, parts_five),
+                (even_older, odd_older, taps_three, mixed_three, three, select_three, parts_three),
             ):
-                out = filtered(even.at[turn], odd.at[turn], taps, kernel, pair, wide, False)
-                for at, lanes, cut in parts(pair, block):
-                    mixed[at, :, lanes] = out[:, cut].astype(BF16)
-
-        each_block(work, span)
+                out = filtered(
+                    even.at[turn], odd.at[turn], taps, kernel, group, select, held.at[odds], False
+                )
+                for pair, row, lanes, value in sides(group, out):
+                    mixed[lax.rem(turn, 2), row] = value.astype(BF16)
 
     def add_taps(turn):
-        def work(pair, block, wide):
-            tap_sums(
-                even_last.at[turn], odd_last.at[turn], even_five.at[turn], sums_five, five, pair, wide
-            )
-            tap_sums(
-                even_older.at[turn], odd_older.at[turn], even_three.at[turn], sums_three, three, pair, wide
-            )
-
-        each_block(work, (0, pairs))
+        for pair in range(pairs):
+            for even, odd, back, folds, gathers, sums, kernel in (
+                (even_last, odd_last, even_five, folds_five, gather_five, sums_five, five),
+                (even_older, odd_older, even_three, folds_three, gather_three, sums_three, three),
+            ):
+                held = folds.at[pair % 2]
+                tap_folds(even.at[turn], odd.at[turn], back.at[turn], held, kernel, pair)
+                sums[...] += jnp.dot(gathers[...], held[...], preferred_element_type=F32)
 
     def add_point(turn, mixed, total):
         flat = mixed[0:height].reshape(-1, channels)
@@ -346,73 +469,148 @@
             device_id_type=MESH,
         )
 
+    pieces = range(len(spans))
+
+    def send(turn, which, part):
+        @pl.when(not_bottom)
+        def _():
+            hop(turn, which, part).start()
+
+    def chain_five(turn):
+        for part in pieces:
+            arrive(turn, 1, part)
+            through_five(turn, outbox.at[turn, 0], spans[part])
+            send(turn, 0, part)
+
+    def chain_three(turn):
+        for part in pieces:
+            through_three(turn, outbox.at[turn, 1], spans[part])
+            send(turn, 1, part)
+
+    def add_points(turn):
+        held = lax.rem(turn, 2)
+        add_point(turn, mixed_three.at[held], total_three)
+        add_point(turn, mixed_five.at[held], total_five)
+
+    def finish_points():
+        for part in pieces:
+            arrive(end, 0, part)
+        for part, mixed, total, give in (
+            (0, mixed_three, total_three, give_three),
+            (1, mixed_five, total_five, give_five),
+        ):
+            add_point(end, mixed.at[end % 2], total)
+            for peer in range(group):
+                give[peer] = (total[peer * rows : (peer + 1) * rows] * factor).astype(BF16)
+            start_share(part)
+
+    side = img // 2
+    mate = img + 1 - 2 * (img % 2)
+    far_inner, far_outer = 2 - side, 3 - 3 * side
+    inner = (img + 1) // 2 % 2 == 1
+    outer = (img + 1) // 2 % 2 == 0
+
+    def pass_on(part, source, slot, sender, peer):
+        target = (take_three, take_five)[part]
+        return pltpu.make_async_remote_copy(
+            src_ref=source,
+            dst_ref=target.at[slot],
+            send_sem=give_sem.at[part, sender],
+            recv_sem=take_sem.at[part, slot],
+            device_id={"sec": sec, "img": peer},
+            device_id_type=MESH,
+        )
+
+    def start_share(part):
+        give = (give_three, give_five)[part]
+        if not folded:
+            for step in range(1, group):
+                share(part, step).start()
+            return
+
+        @pl.when(outer)
+        def _():
+            pass_on(part, give.at[far_outer], 0, 0, mate).start()
+            pass_on(part, give.at[far_inner], 1, 1, mate).start()
+
+        pass_on(part, give.at[mate], 2, 2, mate).start()
+
+    def relay(part):
+        if not folded:
+            return
+        give, take = ((give_three, take_three), (give_five, take_five))[part]
+        held = (relay_three, relay_five)[part]
+
+        @pl.when(inner)
+        def _():
+            for slot, peer in ((0, far_outer), (1, far_inner)):
+                pass_on(part, give.at[peer], slot, slot, mate).wait_recv()
+                held[slot] = (give[peer].astype(F32) + take[slot].astype(F32)).astype(BF16)
+                pass_on(part, held.at[slot], 3, slot, peer).start()
+
     prepare(0)
+    point_both[0:channels] = point_five[...]
+    point_both[channels:] = point_three[...]
+    for ref in (
+        parts_five,
+        parts_three,
+        folds_five,
+        folds_three,
+        sums_five,
+        sums_three,
+        total_five,
+        total_three,
+        sums_all,
+    ):
+        ref[...] = jnp.zeros(ref.shape, ref.dtype)
     callers = group + 1 - bottom.astype(jnp.int32) - top.astype(jnp.int32)
     pl.semaphore_wait(barrier, callers)
-    for ref in (sums_five, sums_three, total_five, total_three, sums_all):
-        ref[...] = jnp.zeros(ref.shape, ref.dtype)
     first_copy(0).wait()
     first_copy(1).wait()
 
     def turn_work(turn, carry):
-        def ready(part):
-            arrive(turn, 1, part)
-            for which, through in ((0, through_five), (1, through_three)):
-                through(turn, outbox.at[turn, which], spans[part])
-
-                @pl.when(not_bottom)
-                def _():
-                    hop(turn, which, part).start()
-
-        for part in range(len(spans)):
+        for part in pieces:
             arrive(turn, 0, part)
-            pull(turn, part)
-            if part > 0:
-                ready(part - 1)
-            if part + 1 < len(spans):
-                forward(turn, spans[part])
-        ready(len(spans) - 1)
-        forward(turn, spans[-1])
-        add_point(turn, mixed_five, total_five)
-        add_point(turn, mixed_three, total_three)
+        pull(turn)
+        chain_five(turn)
+        chain_three(turn)
         prepare(turn + 1)
+
+        def ahead(later, carry):
+            forward(later, (0, pairs))
+            return carry
+
+        lax.fori_loop(turn + lax.min(turn, 1), turn + 2, ahead, 0)
+        add_points(turn)
         return carry
 
     lax.fori_loop(0, end, turn_work, 0)
-
-    forward(end, (0, pairs))
-    for part in range(len(spans)):
-        arrive(end, 0, part)
-    for part, mixed, total, give in (
-        (0, mixed_three, total_three, give_three),
-        (1, mixed_five, total_five, give_five),
-    ):
-        add_point(end, mixed, total)
-        for peer in range(group):
-            give[peer] = (total[peer * rows : (peer + 1) * rows] * factor).astype(BF16)
-        for step in range(1, group):
-            share(part, step).start()
-    for part in range(len(spans)):
-        pull(end, part)
+    finish_points()
+    pull(end)
 
     def all_taps(turn, carry):
+        @pl.when(turn == turns // 2)
+        def _():
+            relay(0)
+
         add_taps(turn)
         return carry
 
     lax.fori_loop(0, turns, all_taps, 0)
+    relay(1)
     count_five, count_three = five * five, three * three
     for sums, start, count in ((sums_five, 0, count_five), (sums_three, count_five, count_three)):
-        folded = jnp.sum(sums[...], axis=1)
-        sums_all[start : start + count] = folded[:, 0:channels] + folded[:, channels:]
+        sums_all[start : start + count] = sums[0:count, 0:channels] + sums[0:count, channels:]
     flipped = sums_all[...].T * factor
     for peer in range(group):
-        give_taps[peer] = flipped[peer * rows : (peer + 1) * rows].astype(BF16)
+        own = flipped[peer * rows : (peer + 1) * rows].T
+        give_taps[peer] = own[0 : give_taps.shape[1]].astype(BF16)
     for step in range(1, group):
         share(2, step).start()
     for part in range(len(spans)):
         arrive(end, 1, part)
-    through_five(end, final.at[0], (0, pairs))
-    through_three(end, final.at[1], (0, pairs))
+    compact_five(end, final.at[0], (0, pairs))
+    compact_three(end, final.at[1], (0, pairs))
     finals = [
         pltpu.make_async_copy(
             final.at[which, pl.ds(0, height)], outgoing.at[which], final_sem.at[which]
@@ -424,6 +622,11 @@
 
     def gathered(part, give, take):
         value = give[img].astype(F32)
+        if folded and part < 2:
+            for slot in (2, 3):
+                pass_on(part, give.at[mate], slot, 2, mate).wait_recv()
+                value = value + take[slot].astype(F32)
+            return value
         for step in range(1, group):
             share(part, step).wait_recv()
             value = value + take[step].astype(F32)
@@ -431,14 +634,18 @@
 
     out_three[...] = gathered(0, give_three, take_three)
     out_five[...] = gathered(1, give_five, take_five)
-    by_tap = gathered(2, give_taps, take_taps).T
+    by_tap = gathered(2, give_taps, take_taps)
     for tap in range(count_five):
         out_taps_five[tap] = by_tap[tap : tap + 1]
     for tap in range(count_three):
         out_taps_three[tap] = by_tap[count_five + tap : count_five + tap + 1]
     for part in range(3):
         for step in range(1, group):
-            share(part, step).wait_send()
+            if folded and part < 2:
+                source = (give_three, give_five)[part].at[mate]
+                pass_on(part, source, 2, step - 1, mate).wait_send()
+            else:
+                share(part, step).wait_send()
     for copy in finals:
         copy.wait()
 
@@ -487,29 +694,35 @@
             jax.ShapeDtypeStruct((count_five, 1, rows), F32),
             jax.ShapeDtypeStruct((count_three, 1, rows), F32),
         ),
-        in_specs=[smem, vmem, vmem, *[outside] * 2, *[vmem] * 4],
+        in_specs=[smem, vmem, vmem, *[outside] * 2, *[vmem] * 10],
         out_specs=(outside, *[vmem] * 4),
         scratch_shapes=[
             pltpu.VMEM((turns, 2, 2 * pairs, breadth, channels), BF16),
             pltpu.VMEM((turns - 1, 2, 2 * pairs, breadth, channels), BF16),
             pltpu.VMEM((2, 2 * pairs, width, channels), BF16),
-            pltpu.VMEM((2 * pairs + 2, breadth, channels), F32),
             *([even, odd] * 4),
-            pltpu.VMEM((2 * pairs, breadth, channels), BF16),
-            pltpu.VMEM((2 * pairs, breadth, channels), BF16),
+            pltpu.VMEM((2, 2 * pairs, breadth, channels), BF16),
+            pltpu.VMEM((2, 2 * pairs, breadth, channels), BF16),
+            pltpu.VMEM((2, TWO * LANES, 2 * channels), BF16),
+            pltpu.VMEM((2, TWO * LANES, 2 * channels), BF16),
+            pltpu.VMEM((2 * channels, channels), BF16),
+            pltpu.VMEM((2, up(count_five * 8, LANES), 2 * channels), BF16),
+            pltpu.VMEM((2, up(count_three * 8, LANES), 2 * channels), BF16),
             pltpu.VMEM((count_five, 8, 2 * channels), BF16),
             pltpu.VMEM((count_three, 8, 2 * channels), BF16),
             pltpu.VMEM((channels, channels), F32),
             pltpu.VMEM((channels, channels), F32),
-            pltpu.VMEM((count_five, 8, 2 * channels), F32),
-            pltpu.VMEM((count_three, 8, 2 * channels), F32),
+            pltpu.VMEM((up(count_five, 8), 2 * channels), F32),
+            pltpu.VMEM((up(count_three, 8), 2 * channels), F32),
             pltpu.VMEM((LANES, channels), F32),
             pltpu.VMEM((group, rows, channels), BF16),
             pltpu.VMEM((group, rows, channels), BF16),
-            pltpu.VMEM((group, rows, LANES), BF16),
+            pltpu.VMEM((group, up(count_five + count_three, 16), rows), BF16),
             pltpu.VMEM((group, rows, channels), BF16),
             pltpu.VMEM((group, rows, channels), BF16),
-            pltpu.VMEM((group, rows, LANES), BF16),
+            pltpu.VMEM((group, up(count_five + count_three, 16), rows), BF16),
+            pltpu.VMEM((2, rows, channels), BF16),
+            pltpu.VMEM((2, rows, channels), BF16),
             pltpu.SemaphoreType.DMA((turns, 2)),
             pltpu.SemaphoreType.DMA((turns - 1, 2, len(spans))),
             pltpu.SemaphoreType.DMA((turns - 1, 2, len(spans))),
@@ -530,6 +743,12 @@
         depth_three[0],
         point_five[0],
         point_three[0],
+        *(
+            selection(breadth, width, kernel, back)
+            for back in (False, True)
+            for kernel in (five, three)
+        ),
+        *(gathering(count) for count in (count_five, count_three)),
     )
     return (
         outgoing.reshape(1, 2, 1, height, width, channels),

time: 57.1 us -> 52.8 us (0.925)
  Pallas kernels: 47.5 us -> 43.1 us
    pallas_call x1, Pallas kernels: 47.5 us -> 43.1 us  [local(): pl.pallas_call(body, out_shape=(jax.ShapeDtypeStruct((2, height, width, c...]
    unnamed x23 -> x35, local copies, waits for them, and re-layouts: 7.93 us -> 7.89 us
where the time goes in v2:
time: 52.8 us; the launch traced here: 52.5 us
  Pallas kernels  43.1 us (82%)
  local copies, waits for them, and re-layouts  8.7 us (16%)
  between operations  0.8 us (2%)
    pallas_call x1, Pallas kernels, local(): pl.pallas_call(body, out_shape=(jax.ShapeDtypeStruct((2, height, width, c...  43.1 us
    unnamed x35, local copies, waits for them, and re-layouts  7.89 us

profile of v2, /device:TPU:1, one launch (start us, length us, event | category | flops | bytes accessed | tf_op | source)
XLA Modules:
  0.0 52.5 jit_solution(2673602847089915462)
XLA Ops:
  0.6 0.0 copy-start.11
  0.6 1.3 %copy.30 = bf16[1,2,1,21,21,384]{5,4,3,1,2,0:T(8,128)(2,1)S(1)} copy(bf16[1,2,1,21,21,384]{5,1,4,3,2,0:T(2,128)(2,1)} %param.17) | data formatting | bytes 1354752 | tf_op args[2]
  2.0 0.1 pad.8.arriving
  2.1 0.3 copy-done.11
  2.4 0.3 copy.29
  2.7 0.0 copy-start.12
  2.7 0.0 copy-start.13
  2.8 0.3 pad.9.head
  3.0 1.0 %copy-done.12 = bf16[1,4,1,21,21,384]{5,1,4,3,2,0:T(4,128)(2,1)S(1)} copy-done((bf16[1,4,1,21,21,384]{5,1,4,3,2,0:T(4,128)(2,1)S(1)}, bf16[1,4,1,21,21,384]{5,1,4,3,2,0:T(4,128)(2,1)}, u32[]{:S(2)}) %copy-start.12) | copy-done | bytes 1354776
  4.1 0.4 copy-done.13
  4.5 0.0 copy-start
  4.5 0.0 copy-start.1
  4.5 0.0 copy-start.2
  4.5 0.0 copy-start.3
  4.5 0.0 copy-start.4
  4.5 0.0 copy-start.5
  4.5 0.0 copy-start.6
  4.5 0.0 copy-start.7
  4.5 0.0 copy-start.8
  4.6 0.0 copy-start.9
  4.6 0.0 copy-start.10
  4.6 0.4 copy_bitcast_fusion.1
  5.0 0.4 copy-done
  5.4 0.1 copy-done.1
  5.5 0.0 copy-done.2
  5.5 0.0 copy-done.3
  5.5 0.0 copy-done.4
  5.5 0.0 copy-done.5
  5.5 0.0 copy-done.6
  5.6 0.0 copy-done.7
  5.6 0.0 copy-done.8
  5.6 0.0 copy-done.9
  5.6 0.0 copy-done.10
  5.6 43.1 %shard_map.182 = (bf16[2,21,21,384]{3,2,1,0:T(8,128)(2,1)S(1)}, f32[96,384]{1,0:T(8,128)S(1)}, f32[96,384]{1,0:T(8,128)S(1)}, f32[25,1,96]{2,1,0:T(1,128)S(1)}, f32[9,1,96]{2,1,0:T(1,128)S(1)}) custom-call(s32[1,4]{1,0:T(1,128)S(1)} %copy-done.10, bf16[4,21,21,384]{3,2,1,0:T(8,128)(2,1)S(1)} %get-tuple-element.21.last, ...), custom_call_target="tpu_custom_call" | custom-call | tf_op jit(solution)/shard_map/pallas_call | solution.py:688
  48.7 1.4 %copy.24 = bf16[1,2,1,21,21,384]{5,1,4,3,2,0:T(2,128)(2,1)} copy(bf16[1,2,1,21,21,384]{5,4,3,1,2,0:T(8,128)(2,1)S(1)} %bitcast.19) | data formatting | bytes 1354752
  50.0 0.7 %copy.35 = f32[1,96,384]{2,1,0:T(8,128)} copy(f32[1,96,384]{2,1,0:T(8,128)S(1)} %bitcast.23) | data formatting | bytes 294912
  50.7 0.6 %copy.36 = f32[1,96,25]{1,0,2:T(1,128)} copy(f32[1,96,25]{1,0,2:T(1,128)S(1)} %bitcast.25) | data formatting | bytes 19200
  51.3 0.7 %copy.37 = f32[1,96,384]{2,1,0:T(8,128)} copy(f32[1,96,384]{2,1,0:T(8,128)S(1)} %bitcast.22) | data formatting | bytes 294912
  52.0 0.6 %copy.38 = f32[1,96,9]{1,0,2:T(1,128)} copy(f32[1,96,9]{1,0,2:T(1,128)S(1)} %bitcast.27) | data formatting | bytes 6912
Async XLA Ops:
  0.6 1.8 %copy-start.11 = (bf16[3,2,1,21,21,384]{5,1,4,3,2,0:T(2,128)(2,1)S(1)}, bf16[3,2,1,21,21,384]{5,1,4,3,2,0:T(2,128)(2,1)}, u32[]{:S(2)}) copy-start(bf16[3,2,1,21,21,384]{5,1,4,3,2,0:T(2,128)(2,1)} %param.18) | copy-start | bytes 6096388
  2.7 1.3 %copy-start.12 = (bf16[1,4,1,21,21,384]{5,1,4,3,2,0:T(4,128)(2,1)S(1)}, bf16[1,4,1,21,21,384]{5,1,4,3,2,0:T(4,128)(2,1)}, u32[]{:S(2)}) copy-start(bf16[1,4,1,21,21,384]{5,1,4,3,2,0:T(4,128)(2,1)} %param.16) | copy-start | bytes 4064260
  2.7 1.7 %copy-start.13 = (bf16[1,4,1,21,21,384]{5,1,4,3,2,0:T(4,128)(2,1)S(1)}, bf16[1,4,1,21,21,384]{5,1,4,3,2,0:T(4,128)(2,1)}, u32[]{:S(2)}) copy-start(bf16[1,4,1,21,21,384]{5,1,4,3,2,0:T(4,128)(2,1)} %param.15) | copy-start | bytes 4064260
  4.5 1.0 %copy-start = (bf16[1,384,384]{2,1,0:T(8,128)(2,1)S(1)}, bf16[1,384,384]{2,1,0:T(8,128)(2,1)}, u32[]{:S(2)}) copy-start(bf16[1,384,384]{2,1,0:T(8,128)(2,1)} %param.22) | copy-start | bytes 884740
  4.5 1.0 %copy-start.1 = (bf16[1,384,384]{2,1,0:T(8,128)(2,1)S(1)}, bf16[1,384,384]{2,1,0:T(8,128)(2,1)}, u32[]{:S(2)}) copy-start(bf16[1,384,384]{2,1,0:T(8,128)(2,1)} %param.23) | copy-start | bytes 884740
  4.5 1.0 %copy-start.2 = (bf16[1,25,384]{2,1,0:T(8,128)(2,1)S(1)}, bf16[1,25,384]{2,1,0:T(8,128)(2,1)}, u32[]{:S(2)}) copy-start(bf16[1,25,384]{2,1,0:T(8,128)(2,1)} %param.20) | copy-start | bytes 57604
  4.5 1.0 %copy-start.3 = (bf16[48,256]{1,0:T(8,128)(2,1)S(1)}, bf16[48,256]{1,0:T(8,128)(2,1)}, u32[]{:S(2)}) copy-start(bf16[48,256]{1,0:T(8,128)(2,1)} %constant.18.clone.select_three_back) | copy-start | bytes 73732
  4.5 1.0 %copy-start.4 = (bf16[48,256]{1,0:T(8,128)(2,1)S(1)}, bf16[48,256]{1,0:T(8,128)(2,1)}, u32[]{:S(2)}) copy-start(bf16[48,256]{1,0:T(8,128)(2,1)} %constant.17.clone.select_five_back) | copy-start | bytes 73732
  4.5 1.0 %copy-start.5 = (bf16[48,256]{1,0:T(8,128)(2,1)S(1)}, bf16[48,256]{1,0:T(8,128)(2,1)}, u32[]{:S(2)}) copy-start(bf16[48,256]{1,0:T(8,128)(2,1)} %constant.16.clone.select_three) | copy-start | bytes 73732
  4.5 1.0 %copy-start.6 = (bf16[48,256]{1,0:T(8,128)(2,1)S(1)}, bf16[48,256]{1,0:T(8,128)(2,1)}, u32[]{:S(2)}) copy-start(bf16[48,256]{1,0:T(8,128)(2,1)} %constant.15.clone.select_five) | copy-start | bytes 73732
  4.5 1.0 %copy-start.7 = (bf16[32,256]{1,0:T(8,128)(2,1)S(1)}, bf16[32,256]{1,0:T(8,128)(2,1)}, u32[]{:S(2)}) copy-start(bf16[32,256]{1,0:T(8,128)(2,1)} %constant.19.clone.gather_five) | copy-start | bytes 49156
  4.5 1.0 %copy-start.8 = (bf16[1,9,384]{2,1,0:T(8,128)(2,1)S(1)}, bf16[1,9,384]{2,1,0:T(8,128)(2,1)}, u32[]{:S(2)}) copy-start(bf16[1,9,384]{2,1,0:T(8,128)(2,1)} %param.21) | copy-start | bytes 20740
  4.6 1.0 %copy-start.9 = (bf16[16,128]{1,0:T(8,128)(2,1)S(1)}, bf16[16,128]{1,0:T(8,128)(2,1)}, u32[]{:S(2)}) copy-start(bf16[16,128]{1,0:T(8,128)(2,1)} %constant.20.clone.gather_three) | copy-start | bytes 12292
  4.6 1.0 %copy-start.10 = (s32[1,4]{1,0:T(1,128)S(1)}, s32[1,4]{1,0:T(1,128)}, u32[]{:S(2)}) copy-start(s32[1,4]{1,0:T(1,128)} %plan.1) | copy-start | bytes 52

commit v3 on v2

--- a/solution.py
+++ b/solution.py
@@ -156,10 +156,8 @@
     gather_five,
     gather_three,
     outgoing,
-    out_five,
-    out_three,
-    out_taps_five,
-    out_taps_three,
+    out_points,
+    out_taps,
     inbox,
     outbox,
     final,
@@ -199,12 +197,12 @@
     give_sem,
     take_sem,
     final_sem,
+    weight_sem,
 ):
     five, three = kernels
     turns, height, width, channels = last.shape
     breadth = inbox.shape[3]
     rows = channels // group
-    factor = 1.0 / (height * width)
     pairs = spans[-1][1]
     blocks = 2 * channels // WIDE
     columns = channels // LANES
@@ -222,21 +220,29 @@
 
     def first_copy(which):
         target = inbox.at[0, which, pl.ds(0, height)]
-        return pltpu.make_async_copy(arriving.at[which], target, local_sem.at[0, which])
-
-    def head_copy(turn, which):
-        source = head.at[turn - 1, which]
-        target = inbox.at[turn, which, pl.ds(0, height)]
-        return pltpu.make_async_copy(source, target, local_sem.at[turn, which])
-
+        return pltpu.make_async_copy(arriving.at[which], target, local_sem.at[which])
+
+    def take_head(turn):
+        edge = jnp.zeros((breadth - width, channels), F32)
+
+        def one(row, carry):
+            both = head[turn - 1, row].astype(F32)
+            for which in range(2):
+                own = both[:, which]
+                inbox[turn, which, row] = jnp.concatenate([own, edge], 0).astype(BF16)
+            return carry
+
+        lax.fori_loop(0, height, one, 0, unroll=3)
+
+    weights = [
+        pltpu.make_async_copy(
+            source, point_both.at[pl.ds(at * channels, channels)], weight_sem.at[at]
+        )
+        for at, source in enumerate((point_five, point_three))
+    ]
     for which in range(2):
         first_copy(which).start()
-
-    @pl.when(top)
-    def _():
-        for turn in range(1, turns):
-            for which in range(2):
-                head_copy(turn, which).start()
+        weights[which].start()
 
     barrier = pltpu.get_barrier_semaphore()
     for step in range(1, group):
@@ -305,11 +311,11 @@
         )
 
     def arrive(turn, which, part):
-        if part == 0:
+        if which == 0 and part == 0:
 
             @pl.when(jnp.logical_and(turn > 0, top))
             def _():
-                head_copy(turn, which).wait()
+                take_head(turn)
 
         @pl.when(jnp.logical_and(turn > 0, not_top))
         def _():
@@ -501,8 +507,15 @@
         ):
             add_point(end, mixed.at[end % 2], total)
             for peer in range(group):
-                give[peer] = (total[peer * rows : (peer + 1) * rows] * factor).astype(BF16)
+                give[peer] = total[peer * rows : (peer + 1) * rows].astype(BF16)
             start_share(part)
+
+        if folded:
+
+            @pl.when(outer)
+            def _():
+                pass_on(0, give_three.at[mate], 2, 2, mate).start()
+                pass_on(1, give_five.at[mate], 2, 2, mate).start()
 
     side = img // 2
     mate = img + 1 - 2 * (img % 2)
@@ -533,7 +546,9 @@
             pass_on(part, give.at[far_outer], 0, 0, mate).start()
             pass_on(part, give.at[far_inner], 1, 1, mate).start()
 
-        pass_on(part, give.at[mate], 2, 2, mate).start()
+        @pl.when(inner)
+        def _():
+            pass_on(part, give.at[mate], 2, 2, mate).start()
 
     def relay(part):
         if not folded:
@@ -549,24 +564,13 @@
                 pass_on(part, held.at[slot], 3, slot, peer).start()
 
     prepare(0)
-    point_both[0:channels] = point_five[...]
-    point_both[channels:] = point_three[...]
-    for ref in (
-        parts_five,
-        parts_three,
-        folds_five,
-        folds_three,
-        sums_five,
-        sums_three,
-        total_five,
-        total_three,
-        sums_all,
-    ):
+    for ref in (parts_five, parts_three):
         ref[...] = jnp.zeros(ref.shape, ref.dtype)
     callers = group + 1 - bottom.astype(jnp.int32) - top.astype(jnp.int32)
     pl.semaphore_wait(barrier, callers)
-    first_copy(0).wait()
-    first_copy(1).wait()
+    for which in range(2):
+        first_copy(which).wait()
+        weights[which].wait()
 
     def turn_work(turn, carry):
         for part in pieces:
@@ -574,6 +578,20 @@
         pull(turn)
         chain_five(turn)
         chain_three(turn)
+
+        @pl.when(turn == 0)
+        def _():
+            for ref in (
+                folds_five,
+                folds_three,
+                sums_five,
+                sums_three,
+                total_five,
+                total_three,
+                sums_all,
+            ):
+                ref[...] = jnp.zeros(ref.shape, ref.dtype)
+
         prepare(turn + 1)
 
         def ahead(later, carry):
@@ -601,7 +619,7 @@
     count_five, count_three = five * five, three * three
     for sums, start, count in ((sums_five, 0, count_five), (sums_three, count_five, count_three)):
         sums_all[start : start + count] = sums[0:count, 0:channels] + sums[0:count, channels:]
-    flipped = sums_all[...].T * factor
+    flipped = sums_all[...].T
     for peer in range(group):
         own = flipped[peer * rows : (peer + 1) * rows].T
         give_taps[peer] = own[0 : give_taps.shape[1]].astype(BF16)
@@ -632,13 +650,11 @@
             value = value + take[step].astype(F32)
         return value
 
-    out_three[...] = gathered(0, give_three, take_three)
-    out_five[...] = gathered(1, give_five, take_five)
+    out_points[1] = gathered(0, give_three, take_three)
+    out_points[0] = gathered(1, give_five, take_five)
     by_tap = gathered(2, give_taps, take_taps)
-    for tap in range(count_five):
-        out_taps_five[tap] = by_tap[tap : tap + 1]
-    for tap in range(count_three):
-        out_taps_three[tap] = by_tap[count_five + tap : count_five + tap + 1]
+    for tap in range(count_five + count_three):
+        out_taps[tap] = by_tap[tap : tap + 1]
     for part in range(3):
         for step in range(1, group):
             if folded and part < 2:
@@ -655,6 +671,14 @@
             for which in range(2):
                 for part in range(len(spans)):
                     hop(turn, which, part).wait_send()
+
+
+def scale_body(factor, points, taps, five, three, taps_five, taps_three):
+    count = taps_five.shape[0]
+    five[...] = points[0] * factor
+    three[...] = points[1] * factor
+    taps_five[...] = taps[0:count] * factor
+    taps_three[...] = taps[count:] * factor
 
 
 def local(
@@ -678,24 +702,24 @@
     even = pltpu.VMEM((turns, pairs + 2, breadth, 2 * channels), BF16)
     odd = pltpu.VMEM((turns, pairs + 1, breadth, 2 * channels), BF16)
     rows = channels // group
+    factor = 1.0 / (height * width)
     chunk = -(-pairs // CHUNKS)
     spans = tuple((at, min(at + chunk, pairs)) for at in range(0, pairs, chunk))
     vmem = pl.BlockSpec(memory_space=pltpu.VMEM)
     smem = pl.BlockSpec(memory_space=pltpu.SMEM)
     outside = pl.BlockSpec(memory_space=pl.ANY)
+    fixed = pl.BlockSpec(memory_space=pltpu.HBM)
     body = functools.partial(kernel_body, sections, group, (five, three), spans)
     grow = (0, breadth - width)
-    outgoing, grad_five, grad_three, taps_five, taps_three = pl.pallas_call(
+    outgoing, points, taps = pl.pallas_call(
         body,
         out_shape=(
             jax.ShapeDtypeStruct((2, height, width, channels), BF16),
-            jax.ShapeDtypeStruct((rows, channels), F32),
-            jax.ShapeDtypeStruct((rows, channels), F32),
-            jax.ShapeDtypeStruct((count_five, 1, rows), F32),
-            jax.ShapeDtypeStruct((count_three, 1, rows), F32),
+            jax.ShapeDtypeStruct((2, rows, channels), F32),
+            jax.ShapeDtypeStruct((count_five + count_three, 1, rows), F32),
         ),
-        in_specs=[smem, vmem, vmem, *[outside] * 2, *[vmem] * 10],
-        out_specs=(outside, *[vmem] * 4),
+        in_specs=[smem, vmem, vmem, outside, vmem, *[vmem] * 2, *[fixed] * 2, *[vmem] * 6],
+        out_specs=(outside, *[vmem] * 2),
         scratch_shapes=[
             pltpu.VMEM((turns, 2, 2 * pairs, breadth, channels), BF16),
             pltpu.VMEM((turns - 1, 2, 2 * pairs, breadth, channels), BF16),
@@ -723,11 +747,12 @@
             pltpu.VMEM((group, up(count_five + count_three, 16), rows), BF16),
             pltpu.VMEM((2, rows, channels), BF16),
             pltpu.VMEM((2, rows, channels), BF16),
-            pltpu.SemaphoreType.DMA((turns, 2)),
+            pltpu.SemaphoreType.DMA((2,)),
             pltpu.SemaphoreType.DMA((turns - 1, 2, len(spans))),
             pltpu.SemaphoreType.DMA((turns - 1, 2, len(spans))),
             pltpu.SemaphoreType.DMA((3, group)),
             pltpu.SemaphoreType.DMA((3, group)),
+            pltpu.SemaphoreType.DMA((2,)),
             pltpu.SemaphoreType.DMA((2,)),
         ],
         compiler_params=pltpu.CompilerParams(
@@ -738,7 +763,7 @@
         saved_last.reshape(turns, height, width, channels),
         saved_older.reshape(turns, height, width, channels),
         jnp.pad(arriving[0, :, 0], ((0, 0), (0, 0), grow, (0, 0))),
-        jnp.pad(head_adjoint[:, :, 0], ((0, 0), (0, 0), (0, 0), grow, (0, 0))),
+        head_adjoint[:, :, 0].transpose(0, 2, 3, 1, 4),
         depth_five[0],
         depth_three[0],
         point_five[0],
@@ -750,6 +775,18 @@
         ),
         *(gathering(count) for count in (count_five, count_three)),
     )
+    grad_five, grad_three, taps_five, taps_three = pl.pallas_call(
+        functools.partial(scale_body, factor),
+        out_shape=(
+            jax.ShapeDtypeStruct((rows, channels), F32),
+            jax.ShapeDtypeStruct((rows, channels), F32),
+            jax.ShapeDtypeStruct((count_five, 1, rows), F32),
+            jax.ShapeDtypeStruct((count_three, 1, rows), F32),
+        ),
+        in_specs=[vmem, vmem],
+        out_specs=(vmem,) * 4,
+        compiler_params=pltpu.CompilerParams(vmem_limit_bytes=GRANT),
+    )(points, taps)
     return (
         outgoing.reshape(1, 2, 1, height, width, channels),
         grad_five[None],

time: 52.8 us -> 49.6 us (0.939)
  local copies, waits for them, and re-layouts: 8.7 us -> 4.9 us
  Pallas kernels: 43.1 us -> 43.8 us
    unnamed x35 -> x30, local copies, waits for them, and re-layouts: 7.89 us -> 4.37 us
    pallas_call x0 -> x1, Pallas kernels: none -> 0.76 us  [local(): pl.pallas_call(functools.partial(scale_body, factor), out_shape=(jax.Shap...]
where the time goes in v3:
time: 49.6 us; the launch traced here: 49.5 us
  Pallas kernels  43.8 us (88%)
  local copies, waits for them, and re-layouts  4.9 us (10%)
  between operations  0.79 us (2%)
    pallas_call x1, Pallas kernels, local(): pl.pallas_call(body, out_shape=(jax.ShapeDtypeStruct((2, height, width, c...  43 us
    unnamed x30, local copies, waits for them, and re-layouts  4.37 us

profile of v3, /device:TPU:1, one launch (start us, length us, event | category | flops | bytes accessed | tf_op | source)
XLA Modules:
  0.0 49.5 jit_solution(13868892572225335580)
XLA Ops:
  0.6 0.0 copy-start.12
  0.6 0.0 copy-start.13
  0.7 1.4 %copy.27 = bf16[1,2,1,21,21,384]{5,4,3,1,2,0:T(8,128)(2,1)S(1)} copy(bf16[1,2,1,21,21,384]{5,1,4,3,2,0:T(2,128)(2,1)} %param.17) | data formatting | bytes 1354752 | tf_op args[2]
  2.0 0.1 pad.4.arriving
  2.1 0.1 copy-done.12
  2.2 0.4 copy-done.13
  2.6 0.0 copy-start
  2.6 0.0 copy-start.1
  2.6 0.0 copy-start.2
  2.6 0.0 copy-start.3
  2.6 0.0 copy-start.4
  2.6 0.0 copy-start.5
  2.6 0.0 copy-start.6
  2.6 0.0 copy-start.7
  2.6 0.0 copy-start.8
  2.7 0.0 copy-start.9
  2.7 0.0 copy-start.10
  2.7 0.0 copy-start.11
  2.7 0.4 copy_bitcast_fusion
  3.1 1.0 %copy-done = bf16[3,2,1,21,21,384]{5,1,4,3,2,0:T(2,128)(2,1)S(1)} copy-done((bf16[3,2,1,21,21,384]{5,1,4,3,2,0:T(2,128)(2,1)S(1)}, bf16[3,2,1,21,21,384]{5,1,4,3,2,0:T(2,128)(2,1)}, u32[]{:S(2)}) %copy-start) | copy-done | bytes 2032152
  4.1 0.0 copy-done.1
  4.2 0.1 copy-done.2
  4.2 0.0 copy-done.3
  4.2 0.0 copy-done.4
  4.2 0.0 copy-done.5
  4.2 0.0 copy-done.6
  4.3 0.0 copy-done.7
  4.3 0.0 copy-done.8
  4.3 0.0 copy-done.9
  4.3 0.0 copy-done.10
  4.3 0.0 copy-done.11
  4.3 43.0 %shard_map.182 = (bf16[2,21,21,384]{3,2,1,0:T(8,128)(2,1)S(1)}, f32[2,96,384]{2,1,0:T(8,128)S(1)}, f32[34,1,96]{2,1,0:T(1,128)S(1)}) custom-call(s32[1,4]{1,0:T(1,128)S(1)} %copy-done.11, bf16[4,21,21,384]{3,2,1,0:T(8,128)(2,1)S(1)} %get-tuple-element.25.last, bf16[4,21,21,384]{3,2,1,0:T(8,128)(2,1)S(1)} %get-tuple-element.24.older, ...), custom_call_target="tpu_custom_call" | custom-call | tf_op jit(solution)/shard_map/pallas_call | solution.py:714
  47.3 1.4 %copy.23 = bf16[1,2,1,21,21,384]{5,1,4,3,2,0:T(2,128)(2,1)} copy(bf16[1,2,1,21,21,384]{5,4,3,1,2,0:T(8,128)(2,1)S(1)} %bitcast.20) | data formatting | bytes 1354752
  48.7 0.8 %shard_map.183 = (f32[96,384]{1,0:T(8,128)}, f32[96,384]{1,0:T(8,128)}, f32[25,1,96]{2,1,0:T(1,128)}, f32[9,1,96]{2,1,0:T(1,128)}) custom-call(f32[2,96,384]{2,1,0:T(8,128)S(1)} %get-tuple-element.13.points, f32[34,1,96]{2,1,0:T(1,128)S(1)} %get-tuple-element.14.taps), custom_call_target="tpu_custom_call" | custom-call | tf_op jit(solution)/shard_map/pallas_call | solution.py:778
Async XLA Ops:
  0.6 1.5 %copy-start.12 = (bf16[1,4,1,21,21,384]{5,1,4,3,2,0:T(4,128)(2,1)S(1)}, bf16[1,4,1,21,21,384]{5,1,4,3,2,0:T(4,128)(2,1)}, u32[]{:S(2)}) copy-start(bf16[1,4,1,21,21,384]{5,1,4,3,2,0:T(4,128)(2,1)} %param.16) | copy-start | bytes 4064260
  0.6 1.9 %copy-start.13 = (bf16[1,4,1,21,21,384]{5,1,4,3,2,0:T(4,128)(2,1)S(1)}, bf16[1,4,1,21,21,384]{5,1,4,3,2,0:T(4,128)(2,1)}, u32[]{:S(2)}) copy-start(bf16[1,4,1,21,21,384]{5,1,4,3,2,0:T(4,128)(2,1)} %param.15) | copy-start | bytes 4064260
  2.6 1.6 %copy-start = (bf16[3,2,1,21,21,384]{5,1,4,3,2,0:T(2,128)(2,1)S(1)}, bf16[3,2,1,21,21,384]{5,1,4,3,2,0:T(2,128)(2,1)}, u32[]{:S(2)}) copy-start(bf16[3,2,1,21,21,384]{5,1,4,3,2,0:T(2,128)(2,1)} %param.18) | copy-start | bytes 6096388
  2.6 1.6 %copy-start.1 = (bf16[1,384,384]{2,1,0:T(8,128)(2,1)S(1)}, bf16[1,384,384]{2,1,0:T(8,128)(2,1)}, u32[]{:S(2)}) copy-start(bf16[1,384,384]{2,1,0:T(8,128)(2,1)} %param.22) | copy-start | bytes 884740
  2.6 1.7 %copy-start.2 = (bf16[1,384,384]{2,1,0:T(8,128)(2,1)S(1)}, bf16[1,384,384]{2,1,0:T(8,128)(2,1)}, u32[]{:S(2)}) copy-start(bf16[1,384,384]{2,1,0:T(8,128)(2,1)} %param.23) | copy-start | bytes 884740
  2.6 1.7 %copy-start.3 = (bf16[1,25,384]{2,1,0:T(8,128)(2,1)S(1)}, bf16[1,25,384]{2,1,0:T(8,128)(2,1)}, u32[]{:S(2)}) copy-start(bf16[1,25,384]{2,1,0:T(8,128)(2,1)} %param.20) | copy-start | bytes 57604
  2.6 1.7 %copy-start.4 = (bf16[48,256]{1,0:T(8,128)(2,1)S(1)}, bf16[48,256]{1,0:T(8,128)(2,1)}, u32[]{:S(2)}) copy-start(bf16[48,256]{1,0:T(8,128)(2,1)} %constant.18.clone.select_three_back) | copy-start | bytes 73732
  2.6 1.6 %copy-start.5 = (bf16[48,256]{1,0:T(8,128)(2,1)S(1)}, bf16[48,256]{1,0:T(8,128)(2,1)}, u32[]{:S(2)}) copy-start(bf16[48,256]{1,0:T(8,128)(2,1)} %constant.17.clone.select_five_back) | copy-start | bytes 73732
  2.6 1.6 %copy-start.6 = (bf16[48,256]{1,0:T(8,128)(2,1)S(1)}, bf16[48,256]{1,0:T(8,128)(2,1)}, u32[]{:S(2)}) copy-start(bf16[48,256]{1,0:T(8,128)(2,1)} %constant.16.clone.select_three) | copy-start | bytes 73732
  2.6 1.6 %copy-start.7 = (bf16[48,256]{1,0:T(8,128)(2,1)S(1)}, bf16[48,256]{1,0:T(8,128)(2,1)}, u32[]{:S(2)}) copy-start(bf16[48,256]{1,0:T(8,128)(2,1)} %constant.15.clone.select_five) | copy-start | bytes 73732
  2.6 1.6 %copy-start.8 = (bf16[32,256]{1,0:T(8,128)(2,1)S(1)}, bf16[32,256]{1,0:T(8,128)(2,1)}, u32[]{:S(2)}) copy-start(bf16[32,256]{1,0:T(8,128)(2,1)} %constant.19.clone.gather_five) | copy-start | bytes 49156
  2.7 1.6 %copy-start.9 = (bf16[1,9,384]{2,1,0:T(8,128)(2,1)S(1)}, bf16[1,9,384]{2,1,0:T(8,128)(2,1)}, u32[]{:S(2)}) copy-start(bf16[1,9,384]{2,1,0:T(8,128)(2,1)} %param.21) | copy-start | bytes 20740
  2.7 1.6 %copy-start.10 = (bf16[16,128]{1,0:T(8,128)(2,1)S(1)}, bf16[16,128]{1,0:T(8,128)(2,1)}, u32[]{:S(2)}) copy-start(bf16[16,128]{1,0:T(8,128)(2,1)} %constant.20.clone.gather_three) | copy-start | bytes 12292
  2.7 1.6 %copy-start.11 = (s32[1,4]{1,0:T(1,128)S(1)}, s32[1,4]{1,0:T(1,128)}, u32[]{:S(2)}) copy-start(s32[1,4]{1,0:T(1,128)} %plan.1) | copy-start | bytes 52

commit v4 on v3

--- a/solution.py
+++ b/solution.py
@@ -15,7 +15,7 @@
 MESH = pl.DeviceIdType.MESH
 TWO = 2
 CHUNKS = 3
-GRANT = 36 * 2**20
+GRANT = 40 * 2**20
 
 
 def up(value, unit):
@@ -198,6 +198,8 @@
     take_sem,
     final_sem,
     weight_sem,
+    raw,
+    head_sem,
 ):
     five, three = kernels
     turns, height, width, channels = last.shape
@@ -222,11 +224,20 @@
         target = inbox.at[0, which, pl.ds(0, height)]
         return pltpu.make_async_copy(arriving.at[which], target, local_sem.at[which])
 
+    def head_copy(turn):
+        return pltpu.make_async_copy(head.at[turn - 1], raw.at[turn - 1], head_sem.at[turn - 1])
+
+    @pl.when(top)
+    def _():
+        for turn in range(1, turns):
+            head_copy(turn).start()
+
     def take_head(turn):
         edge = jnp.zeros((breadth - width, channels), F32)
+        head_copy(turn).wait()
 
         def one(row, carry):
-            both = head[turn - 1, row].astype(F32)
+            both = raw[turn - 1, row].astype(F32)
             for which in range(2):
                 own = both[:, which]
                 inbox[turn, which, row] = jnp.concatenate([own, edge], 0).astype(BF16)
@@ -567,15 +578,19 @@
     for ref in (parts_five, parts_three):
         ref[...] = jnp.zeros(ref.shape, ref.dtype)
     callers = group + 1 - bottom.astype(jnp.int32) - top.astype(jnp.int32)
-    pl.semaphore_wait(barrier, callers)
     for which in range(2):
         first_copy(which).wait()
         weights[which].wait()
+    pull(0)
+    pl.semaphore_wait(barrier, callers)
 
     def turn_work(turn, carry):
-        for part in pieces:
-            arrive(turn, 0, part)
-        pull(turn)
+        @pl.when(turn > 0)
+        def _():
+            for part in pieces:
+                arrive(turn, 0, part)
+            pull(turn)
+
         chain_five(turn)
         chain_three(turn)
 
@@ -709,6 +724,9 @@
     smem = pl.BlockSpec(memory_space=pltpu.SMEM)
     outside = pl.BlockSpec(memory_space=pl.ANY)
     fixed = pl.BlockSpec(memory_space=pltpu.HBM)
+    in_hbm = functools.partial(
+        pltpu.with_memory_space_constraint, memory_space=pltpu.HBM
+    )
     body = functools.partial(kernel_body, sections, group, (five, three), spans)
     grow = (0, breadth - width)
     outgoing, points, taps = pl.pallas_call(
@@ -718,7 +736,7 @@
             jax.ShapeDtypeStruct((2, rows, channels), F32),
             jax.ShapeDtypeStruct((count_five + count_three, 1, rows), F32),
         ),
-        in_specs=[smem, vmem, vmem, outside, vmem, *[vmem] * 2, *[fixed] * 2, *[vmem] * 6],
+        in_specs=[smem, vmem, vmem, outside, fixed, *[vmem] * 2, *[fixed] * 2, *[vmem] * 6],
         out_specs=(outside, *[vmem] * 2),
         scratch_shapes=[
             pltpu.VMEM((turns, 2, 2 * pairs, breadth, channels), BF16),
@@ -754,6 +772,8 @@
             pltpu.SemaphoreType.DMA((3, group)),
             pltpu.SemaphoreType.DMA((2,)),
             pltpu.SemaphoreType.DMA((2,)),
+            pltpu.VMEM((turns - 1, height, width, 2, channels), BF16),
+            pltpu.SemaphoreType.DMA((turns - 1,)),
         ],
         compiler_params=pltpu.CompilerParams(
             collective_id=0, has_side_effects=True, vmem_limit_bytes=GRANT
@@ -763,11 +783,11 @@
         saved_last.reshape(turns, height, width, channels),
         saved_older.reshape(turns, height, width, channels),
         jnp.pad(arriving[0, :, 0], ((0, 0), (0, 0), grow, (0, 0))),
-        head_adjoint[:, :, 0].transpose(0, 2, 3, 1, 4),
+        in_hbm(head_adjoint[:, :, 0].transpose(0, 2, 3, 1, 4)),
         depth_five[0],
         depth_three[0],
-        point_five[0],
-        point_three[0],
+        in_hbm(point_five[0]),
+        in_hbm(point_three[0]),
         *(
             selection(breadth, width, kernel, back)
             for back in (False, True)

time: 49.6 us -> 48.9 us (0.986)
  local copies, waits for them, and re-layouts: 4.9 us -> 4.06 us
    unnamed x30 -> x24, local copies, waits for them, and re-layouts: 4.37 us -> 3.52 us
where the time goes in v4:
time: 48.9 us; the launch traced here: 48.7 us
  Pallas kernels  43.9 us (90%)
  local copies, waits for them, and re-layouts  4.06 us (8%)
  between operations  0.73 us (1%)
    pallas_call x1, Pallas kernels, local(): pl.pallas_call(body, out_shape=(jax.ShapeDtypeStruct((2, height, width, c...  43.2 us
    unnamed x24, local copies, waits for them, and re-layouts  3.52 us

profile of v4, /device:TPU:1, one launch (start us, length us, event | category | flops | bytes accessed | tf_op | source)
XLA Modules:
  0.0 48.7 jit_solution(7930533116146006178)
XLA Ops:
  0.6 0.0 copy-start.9
  0.6 0.0 copy-start.10
  0.7 1.4 %copy.27 = bf16[1,2,1,21,21,384]{5,4,3,1,2,0:T(8,128)(2,1)S(1)} copy(bf16[1,2,1,21,21,384]{5,1,4,3,2,0:T(2,128)(2,1)} %param.17) | data formatting | bytes 1354752 | tf_op args[2]
  2.0 0.1 pad.4.arriving
  2.1 0.1 copy-done.9
  2.2 0.4 copy-done.10
  2.6 0.0 copy-start
  2.6 0.0 copy-start.1
  2.6 0.0 copy-start.2
  2.6 0.0 copy-start.3
  2.6 0.0 copy-start.4
  2.6 0.0 copy-start.5
  2.6 0.0 copy-start.6
  2.6 0.0 copy-start.7
  2.6 0.0 copy-start.8
  2.7 0.4 copy_bitcast_fusion
  3.1 0.2 copy-done
  3.3 0.0 copy-done.1
  3.3 0.0 copy-done.2
  3.4 0.0 copy-done.3
  3.4 0.0 copy-done.4
  3.4 0.0 copy-done.5
  3.4 0.0 copy-done.6
  3.4 0.0 copy-done.7
  3.4 0.0 copy-done.8
  3.4 43.2 %shard_map.182 = (bf16[2,21,21,384]{3,2,1,0:T(8,128)(2,1)S(1)}, f32[2,96,384]{2,1,0:T(8,128)S(1)}, f32[34,1,96]{2,1,0:T(1,128)S(1)}) custom-call(s32[1,4]{1,0:T(1,128)S(1)} %copy-done.8, bf16[4,21,21,384]{3,2,1,0:T(8,128)(2,1)S(1)} %get-tuple-element.25.last, bf16[4,21,21,384]{3,2,1,0:T(8,128)(2,1)S(1)} %get-tuple-element.24.older, ...), custom_call_target="tpu_custom_call" | custom-call | tf_op jit(solution)/shard_map/pallas_call | solution.py:732
  46.6 1.4 %copy.23 = bf16[1,2,1,21,21,384]{5,1,4,3,2,0:T(2,128)(2,1)} copy(bf16[1,2,1,21,21,384]{5,4,3,1,2,0:T(8,128)(2,1)S(1)} %bitcast.19) | data formatting | bytes 1354752
  47.9 0.8 %shard_map.183 = (f32[96,384]{1,0:T(8,128)}, f32[96,384]{1,0:T(8,128)}, f32[25,1,96]{2,1,0:T(1,128)}, f32[9,1,96]{2,1,0:T(1,128)}) custom-call(f32[2,96,384]{2,1,0:T(8,128)S(1)} %get-tuple-element.13.points, f32[34,1,96]{2,1,0:T(1,128)S(1)} %get-tuple-element.14.taps), custom_call_target="tpu_custom_call" | custom-call | tf_op jit(solution)/shard_map/pallas_call | solution.py:798
Async XLA Ops:
  0.6 1.5 %copy-start.9 = (bf16[1,4,1,21,21,384]{5,1,4,3,2,0:T(4,128)(2,1)S(1)}, bf16[1,4,1,21,21,384]{5,1,4,3,2,0:T(4,128)(2,1)}, u32[]{:S(2)}) copy-start(bf16[1,4,1,21,21,384]{5,1,4,3,2,0:T(4,128)(2,1)} %param.16) | copy-start | bytes 4064260
  0.6 1.9 %copy-start.10 = (bf16[1,4,1,21,21,384]{5,1,4,3,2,0:T(4,128)(2,1)S(1)}, bf16[1,4,1,21,21,384]{5,1,4,3,2,0:T(4,128)(2,1)}, u32[]{:S(2)}) copy-start(bf16[1,4,1,21,21,384]{5,1,4,3,2,0:T(4,128)(2,1)} %param.15) | copy-start | bytes 4064260
  2.6 0.7 %copy-start = (bf16[1,25,384]{2,1,0:T(8,128)(2,1)S(1)}, bf16[1,25,384]{2,1,0:T(8,128)(2,1)}, u32[]{:S(2)}) copy-start(bf16[1,25,384]{2,1,0:T(8,128)(2,1)} %param.20) | copy-start | bytes 57604
  2.6 0.8 %copy-start.1 = (bf16[48,256]{1,0:T(8,128)(2,1)S(1)}, bf16[48,256]{1,0:T(8,128)(2,1)}, u32[]{:S(2)}) copy-start(bf16[48,256]{1,0:T(8,128)(2,1)} %constant.18.clone.select_three_back) | copy-start | bytes 73732
  2.6 0.8 %copy-start.2 = (bf16[48,256]{1,0:T(8,128)(2,1)S(1)}, bf16[48,256]{1,0:T(8,128)(2,1)}, u32[]{:S(2)}) copy-start(bf16[48,256]{1,0:T(8,128)(2,1)} %constant.17.clone.select_five_back) | copy-start | bytes 73732
  2.6 0.8 %copy-start.3 = (bf16[48,256]{1,0:T(8,128)(2,1)S(1)}, bf16[48,256]{1,0:T(8,128)(2,1)}, u32[]{:S(2)}) copy-start(bf16[48,256]{1,0:T(8,128)(2,1)} %constant.16.clone.select_three) | copy-start | bytes 73732
  2.6 0.8 %copy-start.4 = (bf16[48,256]{1,0:T(8,128)(2,1)S(1)}, bf16[48,256]{1,0:T(8,128)(2,1)}, u32[]{:S(2)}) copy-start(bf16[48,256]{1,0:T(8,128)(2,1)} %constant.15.clone.select_five) | copy-start | bytes 73732
  2.6 0.8 %copy-start.5 = (bf16[32,256]{1,0:T(8,128)(2,1)S(1)}, bf16[32,256]{1,0:T(8,128)(2,1)}, u32[]{:S(2)}) copy-start(bf16[32,256]{1,0:T(8,128)(2,1)} %constant.19.clone.gather_five) | copy-start | bytes 49156
  2.6 0.8 %copy-start.6 = (bf16[1,9,384]{2,1,0:T(8,128)(2,1)S(1)}, bf16[1,9,384]{2,1,0:T(8,128)(2,1)}, u32[]{:S(2)}) copy-start(bf16[1,9,384]{2,1,0:T(8,128)(2,1)} %param.21) | copy-start | bytes 20740
  2.6 0.8 %copy-start.7 = (bf16[16,128]{1,0:T(8,128)(2,1)S(1)}, bf16[16,128]{1,0:T(8,128)(2,1)}, u32[]{:S(2)}) copy-start(bf16[16,128]{1,0:T(8,128)(2,1)} %constant.20.clone.gather_three) | copy-start | bytes 12292
  2.6 0.8 %copy-start.8 = (s32[1,4]{1,0:T(1,128)S(1)}, s32[1,4]{1,0:T(1,128)}, u32[]{:S(2)}) copy-start(s32[1,4]{1,0:T(1,128)} %plan.1) | copy-start | bytes 52
